TPU v7x, 512 devices: a whole 4x4x16 slice. The times are simulated.
512 devices in a mesh: vocab: 16 (over z_hi, y, core), dp: 8 (over z_lo), replica: 4 (over x).
Axes of the slice: x: 4, y: 4, z: 16 (z_hi: 2, z_lo: 8; z = z_hi * 8 + z_lo), core: 2. Of those that a mesh axis runs over, the one named last changes fastest.
Arguments:
- hidden: bfloat16 [1024, 4096], P('dp'), may hold values from -6 to 6
- head_weight: bfloat16 [4096, 65536], P('dp', ('vocab', 'replica')), may hold values from -0.09375 to 0.09375
- head_bias: float32 [65536], P(('vocab', 'replica')), may hold values from -2.5 to 2.5
- rep_cotangent: float32 [64, 65536], P('dp', ('vocab', 'replica')), may hold values from -6 to 6
- lengths: int32 [64], P('dp'), may hold values from 1 to 16, 640 in all
Outputs:
- pooled: float32 [64, 65536], P('dp', ('vocab', 'replica'))
- term_mean: float32 [65536], P(('vocab', 'replica'))
- bias_grad: float32 [65536], P(('vocab', 'replica'))
- weight_grad: float32 [4096, 65536], P('dp', ('vocab', 'replica'))
- input_grad: float32 [1024, 4096], P(('vocab', 'replica'), 'dp')
Inputs may be any that keep to these rules, and one draw needn't show every extreme that they name: `lengths`: each sequence has at least one live token; some sequence has all 16 live.
All inputs are finite; a program needn't handle non-finite values. No bound on the sum of `lengths` on one device may be relied on, other than what follows from the above.
Results may differ from a plain program's by a relative error of at most 0.015.
Values may be sent and summed in bfloat16 or wider, within the bound.
No kernel may reach another device: no remote copies, remote signals or barrier semaphores. Data moves between devices by JAX's collectives and lax.ppermute only.
A program may use at most 64 MiB of HBM per device.

v0:
```python
import jax
import jax.numpy as jnp
from jax import lax
from jax.sharding import PartitionSpec as P


def per_device(hidden, head_weight, head_bias, rep_cotangent, lengths):
    tok_rows = hidden.shape[0]
    block = head_weight.shape[0]
    vocab_cols = head_weight.shape[1]
    dp_count = lax.axis_size("dp")
    seq_count = lengths.shape[0]
    seq_len = tok_rows // seq_count
    columns = lax.all_to_all(hidden, "dp", split_axis=1, concat_axis=0, tiled=True)
    running = jnp.zeros((tok_rows, vocab_cols), jnp.float32)
    piece = lax.all_gather(head_weight, "dp", axis=0, tiled=True)
    count = piece.shape[0] // block
    for index in range(count):
        left = lax.dynamic_slice_in_dim(hidden, index * block, block, 1)
        part = jnp.dot(
            left, piece[index * block : (index + 1) * block, :], preferred_element_type=jnp.float32
        ).astype(jnp.bfloat16)
        running = running + lax.optimization_barrier(part).astype(jnp.float32)
    logits = running + head_bias[None, :]
    positive = jnp.maximum(logits, 0.0)
    grid = jnp.log1p(positive).reshape(seq_count, seq_len, vocab_cols)
    live = (jnp.arange(seq_len, dtype=jnp.int32)[None, :] < lengths[:, None]).astype(jnp.float32)[
        :, :, None
    ]
    squared = grid * grid
    total = 1.0 + jnp.sum(live * squared * squared, axis=1)
    pooled = total**0.25 - 1.0
    factor = (
        live
        * squared
        * grid
        * (total ** (-0.75))[:, None, :]
        / (1.0 + positive.reshape(seq_count, seq_len, vocab_cols))
    )
    column_sum = jnp.sum(pooled, axis=0)
    seq_total = seq_count * dp_count
    term_mean = lax.psum(column_sum, "dp") / seq_total
    grad_pooled = rep_cotangent + term_mean[None, :]
    grad_logits = (factor * grad_pooled[:, None, :]).reshape(tok_rows, vocab_cols)
    bias_grad = lax.psum(jnp.sum(grad_logits, axis=0), "dp")
    grad_round = grad_logits.astype(jnp.bfloat16)
    piece = lax.all_gather(grad_round, "dp", axis=0, tiled=True)
    left = columns
    weight_sum_acc = jnp.einsum("tk,tv->kv", left, piece, preferred_element_type=jnp.float32)
    rows_out = jnp.einsum("tv,kv->tk", piece, head_weight, preferred_element_type=jnp.float32)
    input_part = rows_out
    weight_grad, input_part = (weight_sum_acc, input_part)
    input_grad = lax.psum_scatter(input_part, ("vocab", "replica"), scatter_dimension=0, tiled=True)
    return (pooled, term_mean, bias_grad, weight_grad, input_grad)


def solution(mesh):
    placed = (
        P("dp", None),
        P("dp", ("vocab", "replica")),
        P(("vocab", "replica")),
        P("dp", ("vocab", "replica")),
        P("dp"),
    )
    return jax.shard_map(
        per_device,
        mesh=mesh,
        in_specs=placed,
        out_specs=(
            P("dp", ("vocab", "replica")),
            P(("vocab", "replica")),
            P(("vocab", "replica")),
            P("dp", ("vocab", "replica")),
            P(("vocab", "replica"), "dp"),
        ),
        check_vma=False,
    )
```

profile of v0, /device:TPU:64, one launch (start us, length us, event | category | flops | bytes accessed | tf_op | source)
XLA Modules:
  0.0 897.8 jit_solution(8657482168924879488)
XLA Ops:
  7.2 0.7 all-gather.3.cloned.1.call-update
  8.0 0.7 fusion.18
  8.8 180.1 %all-gather.3.cloned.1.call-done = bf16[4096,1024]{1,0:T(8,128)(2,1)} async-done(((bf16[512,1024]{1,0:T(8,128)(2,1)}), bf16[4096,1024]{1,0:T(8,128)(2,1)}) %all-gather.3.cloned.1.call-update) | async-done | bytes 8388624 | tf_op jit(solution)/shard_map/all_gather | solution.py:16
  188.9 1.6 convolution_convert_fusion.7
  190.5 1.6 convolution_convert_fusion.6
  192.1 1.6 convolution_convert_fusion.5
  193.7 1.6 convolution_convert_fusion.4
  195.4 1.6 convolution_convert_fusion.3
  197.0 1.6 convolution_convert_fusion.2
  198.6 1.6 convolution_convert_fusion.1
  200.2 1.6 convolution_convert_fusion
  201.9 0.6 fusion.8
  202.5 0.6 fusion.20
  203.1 26.0 %psum.14 = f32[1024]{0:T(1024)S(1)} all-reduce(f32[1024]{0:T(1024)S(1)} %get-tuple-element.22), channel_id=1, replica_groups=mesh['vocab'=16,'dp'=8,'replica'=4] {'dp'}, use_global_device_ids=true, to_apply=%region_2.0 | all-reduce | flops 1024 | bytes 8192 | tf_op jit(solution)/shard_map/psum | solution.py:42
  229.1 1.0 fusion.19
  230.2 73.2 %all-gather.5.cloned.1.call-done = bf16[1024,1024]{1,0:T(8,128)(2,1)} async-done(((bf16[128,1024]{1,0:T(8,128)(2,1)}), bf16[1024,1024]{1,0:T(8,128)(2,1)}) %all-gather.5.cloned.1.call-update) | async-done | bytes 2097168 | tf_op jit(solution)/shard_map/all_gather | solution.py:47
  303.4 4.2 fusion.21
  307.6 1.6 copy.12
  309.2 59.9 %all_to_all.19 = bf16[128,8,512]{0,2,1:T(8,128)(2,1)S(1)} all-to-all(bf16[128,8,512]{0,2,1:T(8,128)(2,1)S(1)} %bitcast.22), channel_id=1, replica_groups=mesh['vocab'=16,'dp'=8,'replica'=4] {'dp'}, dimensions={1} | all-to-all | bytes 2097152 | tf_op jit(solution)/shard_map/all_to_all | solution.py:14
  369.1 0.5 copy.13
  369.7 23.8 %psum.15 = f32[1024]{0:T(1024)} all-reduce(f32[1024]{0:T(1024)S(1)} %reduce_sum.29), channel_id=1, replica_groups=mesh['vocab'=16,'dp'=8,'replica'=4] {'dp'}, use_global_device_ids=true, to_apply=%region_4.0 | all-reduce | flops 1024 | bytes 8192 | tf_op jit(solution)/shard_map/psum | solution.py:45
  393.5 2.9 convolution_bitcast_fusion
  396.4 1.8 copy.14
  398.2 493.1 %reduce-scatter.2.cloned.1.call-done = f32[16,512]{1,0:T(8,128)} async-done(((f32[1024,512]{1,0:T(8,128)}), f32[16,512]{1,0:T(8,128)}) %reduce-scatter.2.cloned.1.call-update) | async-done | bytes 32784 | tf_op jit(solution)/shard_map/reduce_scatter | solution.py:53
  (17 shorter events, 0.3 us)
Async XLA Ops:
  7.2 194.7 %copy-start.3 = (f32[1024]{0:T(1024)S(1)}, f32[1024]{0:T(1024)}, u32[]{:S(2)}) copy-start(f32[1024]{0:T(1024)} %param.7) | copy-start | bytes 12292
  7.2 221.9 %copy-start.1 = (f32[8,1024]{1,0:T(8,128)S(1)}, f32[8,1024]{1,0:T(8,128)}, u32[]{:S(2)}) copy-start(f32[8,1024]{1,0:T(8,128)} %param.8) | copy-start | bytes 98308
  7.2 181.7 %all-gather.3.cloned.1.call-start = ((), (), s32[]{:S(2)}) async-start(), calls=%async_computation.2 | async-start | bytes 9437184 | tf_op jit(solution)/shard_map/all_gather | solution.py:16
  7.9 295.4 %all-gather.5.cloned.1.call-start = ((), (), s32[]{:S(2)}) async-start(), calls=%async_computation.3 | async-start | bytes 2359296 | tf_op jit(solution)/shard_map/all_gather | solution.py:47
  8.8 294.6 %copy-start = (bf16[512,1024]{1,0:T(8,128)(2,1)S(1)}, bf16[512,1024]{1,0:T(8,128)(2,1)}, u32[]{:S(2)}) copy-start(bf16[512,1024]{1,0:T(8,128)(2,1)} %param.6) | copy-start | bytes 3145732
  229.1 140.0 %copy-start.2 = (f32[1024]{0:T(1024)}, f32[1024]{0:T(1024)S(1)}, u32[]{:S(2)}) copy-start(f32[1024]{0:T(1024)S(1)} %broadcast_multiply_fusion) | copy-start | bytes 12292
  230.1 661.1 %reduce-scatter.2.cloned.1.call-start = ((), (), s32[]{:S(2)}) async-start(), calls=%async_computation.4 | async-start | bytes 2129920 | tf_op jit(solution)/shard_map/reduce_scatter | solution.py:53
Sparse Core Ops, SparseCore 0:
  10.1 178.7 all-gather.2
  230.3 73.0 all-gather.4
  307.7 583.5 reduce-scatter.1
where the time goes:
time: 898 us
  waiting for transfers between devices  747 us (83%)
  blocking collectives  110 us (12%)
  matrix products  20 us (2%)
  between operations  13.9 us (2%)
    reduce_scatter x1, waiting for transfers between devices, per_device(): lax.psum_scatter(input_part, ('vocab', 'replica'), scatter_dimension=0, t...  493 us
    all_gather x1, waiting for transfers between devices, per_device(): piece = lax.all_gather(head_weight, 'dp', axis=0, tiled=True)  180 us
    all_gather x1, waiting for transfers between devices, per_device(): piece = lax.all_gather(grad_round, 'dp', axis=0, tiled=True)  73.2 us
    all_to_all x1, blocking collectives, per_device(): lax.all_to_all(hidden, 'dp', split_axis=1, concat_axis=0, tiled=True)  59.9 us
    psum x1, blocking collectives, per_device(): term_mean = lax.psum(column_sum, 'dp') / seq_total  26 us
    psum x1, blocking collectives, per_device(): bias_grad = lax.psum(jnp.sum(grad_logits, axis=0), 'dp')  23.8 us
  transfers between devices with their start and end apart: 3, of which 3 were waited for; matrix products, arithmetic and copies ran while one was open for 1% of the time, Pallas kernels for 0%

commit v1 on v0

v1 whole, which is shorter than its diff:
```python
import functools

import jax
import jax.numpy as jnp
from jax import lax
from jax.experimental import pallas as pl
from jax.experimental.pallas import tpu as pltpu
from jax.sharding import Mesh
from jax.sharding import PartitionSpec as P


F32 = jnp.float32
BF16 = jnp.bfloat16
I32 = jnp.int32

SEQS = 64
LEN = 16
TOKENS = SEQS * LEN
LIVE = SEQS * LEN * 5 // 8
HALF = LIVE // 2
LANES = 128
CUT = 256
BLOCK = 512
PACK = 176
EXTRA = 32

VMEM = functools.partial(pl.BlockSpec, memory_space=pltpu.VMEM)
SMEM = functools.partial(pl.BlockSpec, memory_space=pltpu.SMEM)


def call(body, outs, ins, flops=0, moved=0, scalars=1):
    return kernel(body, outs, ins, flops, moved, scalars)


def kernel(body, outs, ins, flops, moved, scalars):
    return pl.pallas_call(
        body,
        out_shape=outs,
        in_specs=[SMEM()] * scalars + [VMEM()] * (len(ins) - scalars),
        out_specs=jax.tree.map(lambda _: VMEM(), outs),
        cost_estimate=pl.CostEstimate(flops=flops, bytes_accessed=moved, transcendentals=0),
    )(*ins)


def iota(shape, dim):
    return lax.broadcasted_iota(I32, shape, dim)


def split(value):
    high = value.astype(BF16)
    return high, (value - high.astype(F32)).astype(BF16)


def dot(left, right, dims=((1,), (0,))):
    return lax.dot_general(left, right, (dims, ((), ())), preferred_element_type=F32)


def weights_body(at, w_ref, *outs):
    for m, out in enumerate(outs):
        start = pl.multiple_of((at[0] ^ m) * CUT, CUT)
        out[...] = w_ref[:, pl.ds(start, CUT)]


def packet_body(at, lengths, even_ref, odd_ref, cot_ref, out):
    row = iota((16, LANES), 0)
    lens = jnp.zeros((16, LANES), F32)
    for s in range(8):
        lens = jnp.where(row == s, lengths[s].astype(F32), lens)
    lens = lens.astype(BF16)
    for a in range(4):
        high, low = split(cot_ref[:, a * CUT : (a + 1) * CUT])
        pieces = []
        for part in (high.astype(F32), low.astype(F32)):
            pieces.append(jnp.concatenate([part[:, :LANES], part[:, LANES:]], axis=0).astype(BF16))
        for q, source in enumerate((even_ref, odd_ref)):
            k = 2 * a + q
            out[k, 0:128, :] = source[...]
            out[k, 128:144, :] = lens
            out[k, 144:160, :] = pieces[0]
            out[k, 160:176, :] = pieces[1]


def compact_body(at, got, out, cot_out, len_out):
    column = jnp.concatenate([got[k, 128:144, :].astype(F32)[0:8] for k in range(8)], axis=0)
    len_out[...] = column
    wide = jnp.broadcast_to(column[:, 0:1], (SEQS, TOKENS))
    seq = iota((SEQS, TOKENS), 0)
    token = iota((SEQS, TOKENS), 1)
    start = jnp.sum(jnp.where(seq < token // LEN, wide, 0.0), axis=0, keepdims=True)
    length = jnp.sum(jnp.where(seq == token // LEN, wide, 0.0), axis=0, keepdims=True)
    place = iota((1, TOKENS), 1) % LEN
    spot = jnp.where(place.astype(F32) < length, start.astype(I32) + place, -1)
    rows = iota((HALF, TOKENS), 0) + at[2] * HALF
    pick = jnp.where(jnp.broadcast_to(spot, (HALF, TOKENS)) == rows, 1.0, 0.0).astype(BF16)
    tokens = jnp.concatenate([got[k, 0:128, :] for k in range(8)], axis=0)
    chosen = dot(pick, tokens).astype(BF16)
    for j in range(16):
        out[j] = chosen
    for k in range(8):
        high = got[k, 144:160, :].astype(F32)
        low = got[k, 160:176, :].astype(F32)
        both = high + low
        cot_out[k * 8 : (k + 1) * 8, 0:LANES] = both[0:8]
        cot_out[k * 8 : (k + 1) * 8, LANES:CUT] = both[8:16]


def tables_body(at, len_ref, seg_ref, segt_ref, spread_ref):
    lens = len_ref[...]
    sub = iota((SEQS, LANES), 0)
    lane = iota((SEQS, LANES), 1)
    start_row = jnp.sum(jnp.where(sub < lane, lens, 0.0), axis=0, keepdims=True)
    len_row = jnp.sum(jnp.where(sub == lane, lens, 0.0), axis=0, keepdims=True)
    start_col = jnp.sum(
        jnp.where(lane < sub, jnp.broadcast_to(len_row, (SEQS, LANES)), 0.0), axis=1, keepdims=True
    )
    spot = iota((SEQS, LIVE), 1).astype(F32)
    first = jnp.broadcast_to(start_col, (SEQS, LIVE))
    last = jnp.broadcast_to(start_col + lens[:, 0:1], (SEQS, LIVE))
    seg_ref[...] = jnp.where((spot >= first) & (spot < last), 1.0, 0.0).astype(BF16)
    spot = iota((LIVE, LANES), 0).astype(F32)
    first = jnp.broadcast_to(start_row, (LIVE, LANES))
    last = jnp.broadcast_to(start_row + len_row, (LIVE, LANES))
    inside = (spot >= first) & (spot < last) & (iota((LIVE, LANES), 1) < SEQS)
    segt_ref[...] = jnp.where(inside, 1.0, 0.0).astype(BF16)
    row = iota((TOKENS, LANES), 0)
    lane = iota((TOKENS, LANES), 1)
    core = (row >> 9) ^ at[2]
    which = (((((row >> 4) & 1) * 4 + ((row >> 7) & 3)) * 2 + core) * 4) + ((row >> 5) & 3)
    per_row = jnp.broadcast_to(len_row, (TOKENS, LANES))
    start = jnp.sum(jnp.where(lane < which, per_row, 0.0), axis=1, keepdims=True)
    length = jnp.sum(jnp.where(lane == which, per_row, 0.0), axis=1, keepdims=True)
    place = (row[:, 0:1] & 15).astype(F32)
    spot = jnp.where(place < length, start + place, -1.0)
    target = iota((TOKENS, LIVE), 1).astype(F32)
    spread_ref[...] = jnp.where(jnp.broadcast_to(spot, (TOKENS, LIVE)) == target, 1.0, 0.0).astype(BF16)


def wide_rows(ref, block):
    return jnp.concatenate([ref[block * 4 + i] for i in range(4)], axis=1)


def logits_body(at, own, other, w0, w1, w2, w3, out):
    for hop, ref in enumerate((own, other)):
        total = jnp.zeros((HALF, CUT), F32)
        for m, w in enumerate((w0, w1, w2, w3)):
            total = total + dot(wide_rows(ref, at[0] ^ m), w[...])
        half = at[2] ^ hop
        out[pl.ds(pl.multiple_of(half * HALF, HALF), HALF), :] = total.astype(BF16)


def grads_body(at, mine, theirs, bias, cot, seg, segt, grad_out, x0, x1, x2, x3):
    logits = mine[...].astype(F32) + theirs[...].astype(F32) + bias[pl.ds(at[0], 1), :]
    positive = jnp.maximum(logits, 0.0)
    act = jnp.log1p(positive)
    cube = act * act * act
    high, low = split(cube * act)
    total = 1.0 + (dot(seg[...], high) + dot(seg[...], low))
    second = jnp.sqrt(total)
    fourth = jnp.sqrt(second)
    pooled = fourth - 1.0
    mean = jnp.sum(pooled, axis=0, keepdims=True) / SEQS
    pull = (cot[...] + mean) / (second * fourth)
    pad = jnp.zeros((LANES - SEQS, CUT), BF16)
    high, low = split(pull)
    spread = dot(segt[...], jnp.concatenate([high, pad], axis=0))
    spread = spread + dot(segt[...], jnp.concatenate([low, pad], axis=0))
    grad = spread * (cube / (1.0 + positive))
    bias_grad = jnp.sum(grad, axis=0, keepdims=True)
    grad_out[...] = grad.astype(BF16)
    m_high, m_low = split(mean)
    b_high, b_low = split(bias_grad)
    row = iota((16, CUT), 0)
    tail = jnp.zeros((16, CUT), F32)
    for i, v in enumerate((m_high, m_low, b_high, b_low)):
        tail = jnp.where(row == i, jnp.broadcast_to(v.astype(F32), (16, CUT)), tail)
    tail = tail.astype(BF16)
    for m, out in enumerate((x0, x1, x2, x3)):
        k = (at[0] ^ m) * 2 + at[1]
        mine8 = jnp.zeros((8, CUT), F32)
        for i in range(8):
            mine8 = jnp.where(k == i, pooled[i * 8 : (i + 1) * 8], mine8)
        high, low = split(mine8)
        out[0:16, :] = jnp.concatenate([high.astype(F32), low.astype(F32)], axis=0).astype(BF16)
        out[16:32, :] = tail


def weight_grad_body(at, own, other, grad, x0, x1, x2, x3, o0, o1, o2, o3):
    for m, (extra, out) in enumerate(zip((x0, x1, x2, x3), (o0, o1, o2, o3))):
        total = jnp.zeros((BLOCK, CUT), F32)
        for hop, ref in enumerate((own, other)):
            half = at[2] ^ hop
            part = grad[pl.ds(pl.multiple_of(half * HALF, HALF), HALF), :]
            total = total + dot(wide_rows(ref, at[0] ^ m), part, ((0,), (0,)))
        out[0:BLOCK, :] = total.astype(BF16)
        out[BLOCK : BLOCK + EXTRA, :] = extra[...]


def send_body(at, spread, grad, w0, w1, w2, w3, out):
    rows = dot(spread[TOKENS // 2 :, :], grad[...]).astype(BF16)
    for m, w in enumerate((w0, w1, w2, w3)):
        start = pl.multiple_of((at[0] ^ m) * BLOCK, BLOCK)
        out[:, pl.ds(start, BLOCK)] = dot(rows, w[...], ((1,), (1,))).astype(BF16)


def keep_body(at, spread, grad, w0, w1, w2, w3, got, out):
    rows = dot(spread[: TOKENS // 2, :], grad[...]).astype(BF16)
    for m, w in enumerate((w0, w1, w2, w3)):
        start = pl.multiple_of((at[0] ^ m) * BLOCK, BLOCK)
        part = dot(rows, w[...], ((1,), (1,)))
        out[:, pl.ds(start, BLOCK)] = (part + got[:, pl.ds(start, BLOCK)].astype(F32)).astype(BF16)


def plane_body(got, out):
    total = got[0].astype(F32)
    for i in range(1, 16):
        total = total + got[i].astype(F32)
    total = total.astype(BF16)
    for zh in range(2):
        for a in range(4):
            out[zh * 4 + a] = total[zh * 16 : (zh + 1) * 16, a * BLOCK : (a + 1) * BLOCK]


def last_body(got, out):
    total = got[0].astype(F32)
    for i in range(1, 8):
        total = total + got[i].astype(F32)
    out[...] = total


def unpack_body(at, p0, p1, p2, p3, weight_out, pooled_out, mean_out, bias_out):
    for m, piece in enumerate((p0, p1, p2, p3)):
        columns = pl.ds(pl.multiple_of((at[0] ^ m) * CUT, CUT), CUT)
        weight_out[:, columns] = piece[0:BLOCK, :].astype(F32)
        extra = piece[BLOCK : BLOCK + EXTRA, :].astype(F32)
        pooled_out[:, columns] = extra[0:8] + extra[8:16]
        mean_out[:, columns] = extra[16:17] + extra[17:18]
        bias_out[:, columns] = extra[18:19] + extra[19:20]


def pack(at, lengths, hidden, rep_cotangent):
    return pl.pallas_call(
        packet_body,
        grid_spec=pltpu.PrefetchScalarGridSpec(
            num_scalar_prefetch=2,
            grid=(1,),
            in_specs=[
                pl.BlockSpec((128, LANES), lambda i, at, n: (0, at[4])),
                pl.BlockSpec((128, LANES), lambda i, at, n: (0, at[4] + 4)),
                pl.BlockSpec((8, 1024), lambda i, at, n: (0, 0)),
            ],
            out_specs=pl.BlockSpec((8, PACK, LANES), lambda i, at, n: (0, 0, 0)),
        ),
        out_shape=shape((8, PACK, LANES)),
        name="packet",
    )(at, lengths, hidden, hidden, rep_cotangent)


def shape(dims, kind=BF16):
    return jax.ShapeDtypeStruct(dims, kind)


def per_device(hidden, head_weight, head_bias, rep_cotangent, lengths):
    a, q, c = lax.axis_index("zq"), lax.axis_index("zp"), lax.axis_index("c")
    j = lax.axis_index("y") * 4 + lax.axis_index("x")
    spot = (2 * (j // 4)) * 4 + j % 4
    at = jnp.stack([a, q, c, j, spot, spot, spot, spot]).astype(I32)

    def swap(value, axis, size, m):
        return lax.ppermute(value, axis, [(i, i ^ m) for i in range(size)])

    def trade(value, axes):
        return lax.all_to_all(value, axes, 0, 0, tiled=True)

    w = call(weights_body, [shape((BLOCK, CUT))] * 4, [at, head_weight])
    w = [w[0]] + [swap(w[m], "zq", 4, m) for m in (1, 2, 3)]

    packets = pack(at, lengths, hidden, rep_cotangent)
    got = trade(packets, ("zq", "zp"))
    rows, cot, lens = call(
        compact_body,
        [shape((16, HALF, LANES)), shape((SEQS, CUT), F32), shape((SEQS, LANES), F32)],
        [at, got],
    )
    own = trade(rows, ("y", "x"))
    other = swap(own, "c", 2, 1)
    seg, segt, spread = call(
        tables_body,
        [shape((SEQS, LIVE)), shape((LIVE, LANES)), shape((TOKENS, LIVE))],
        [at, lens],
        flops=10_000_000,
        moved=2_000_000,
    )
    mine = call(
        logits_body, shape((LIVE, CUT)), [at, own, other, *w], 2 * LIVE * 2048 * CUT, 4 << 20
    )
    theirs = swap(mine, "zp", 2, 1)
    grad, *extra = call(
        grads_body,
        [shape((LIVE, CUT))] + [shape((EXTRA, CUT))] * 4,
        [at, mine, theirs, head_bias.reshape(4, CUT), cot, seg, segt],
    )
    send = call(
        send_body, shape((512, 2048)), [at, spread, grad, *w], 2 * 512 * 2048 * CUT, 4 << 20
    )
    came = swap(send, "c", 2, 1)
    pieces = call(
        weight_grad_body,
        [shape((BLOCK + EXTRA, CUT))] * 4,
        [at, own, other, grad, *extra],
        2 * LIVE * 2048 * CUT,
        4 << 20,
    )
    pieces = [pieces[0]] + [swap(pieces[m], "zq", 4, m) for m in (1, 2, 3)]
    kept = call(
        keep_body, shape((512, 2048)), [at, spread, grad, *w, came], 2 * 512 * 2048 * CUT, 6 << 20
    )
    plane = trade(kept.reshape(16, 32, 2048), ("y", "x"))
    column = call(plane_body, shape((8, 16, BLOCK)), [plane], scalars=0)
    column = trade(column, ("zh", "zq"))
    input_grad = call(last_body, shape((16, BLOCK), F32), [column], scalars=0)
    weight_grad, pooled, mean, bias_grad = call(
        unpack_body,
        [shape((BLOCK, 1024), F32), shape((8, 1024), F32), shape((1, 1024), F32), shape((1, 1024), F32)],
        [at, *pieces],
    )
    return pooled, mean.reshape(1024), bias_grad.reshape(1024), weight_grad, input_grad


def solution(mesh):
    fine = Mesh(mesh.devices.reshape(2, 4, 2, 4, 2, 4), ("zh", "y", "c", "zq", "zp", "x"))
    dp = ("zq", "zp")
    columns = ("zh", "y", "c", "x")

    return jax.shard_map(
        per_device,
        mesh=fine,
        in_specs=(P(dp, None), P(dp, columns), P(columns), P(dp, columns), P(dp)),
        out_specs=(P(dp, columns), P(columns), P(columns), P(dp, columns), P(columns, dp)),
        check_vma=False,
    )
```

time: 898 us -> 273 us (0.30)
  waiting for transfers between devices: 747 us -> 99.3 us
  starting transfers between devices: 0.12 us -> 38.4 us
  Pallas kernels: 0 us -> 36.5 us
  matrix products: 20 us -> 0 us
  blocking collectives: 110 us -> 90.9 us
  between operations: 13.9 us -> 0.79 us
    reduce_scatter x1 -> x0, waiting for transfers between devices: 493 us -> none  [per_device(): lax.psum_scatter(input_part, ('vocab', 'replica'), scatter_dimension=0, t...]
    all_gather x2 -> x0, waiting for transfers between devices: 253 us -> none  [the longest x1 180 us: per_device(): piece = lax.all_gather(head_weight, 'dp', axis=0, tiled=True)]
    ppermute x0 -> x9, waiting for transfers between devices: none -> 99.3 us  [swap(): return lax.ppermute(value, axis, [(i, i ^ m) for i in range(size)])]
    psum x2 -> x0, blocking collectives: 49.8 us -> none  [the longest x1 26 us: per_device(): term_mean = lax.psum(column_sum, 'dp') / seq_total]
    pallas_call x0 -> x12, Pallas kernels: none -> 36.5 us  [the longest x11 34.2 us: kernel(): pl.pallas_call(body, out_shape=outs, in_specs=[SMEM()] * scalars + [VMEM(...]
    all_to_all x1 -> x3, blocking collectives: 59.9 us -> 90.9 us  [trade(): return lax.all_to_all(value, axes, 0, 0, tiled=True)]
    ppermute x0 -> x9, starting transfers between devices: none -> 30.3 us  [swap(): return lax.ppermute(value, axis, [(i, i ^ m) for i in range(size)])]
    dot_general x10 -> x0, matrix products: 20 us -> none  [the longest x8 12.9 us: per_device(): jnp.dot(left, piece[index * block:(index + 1) * block, :], preferred_elem...]
  transfers between devices with their start and end apart: 3 -> 10, of which waited for: 3 -> 8; matrix products, arithmetic and copies ran while one was open for 1% -> 0% of each run, Pallas kernels for 0% -> 4%
where the time goes in v1:
time: 273 us; the launch traced here: 272 us
  waiting for transfers between devices  99.3 us (36%)
  blocking collectives  90.9 us (33%)
  starting transfers between devices  38.4 us (14%)
  Pallas kernels  36.5 us (13%)
  local copies, waits for them, and re-layouts  5.84 us (2%)
    ppermute x9, waiting for transfers between devices, swap(): return lax.ppermute(value, axis, [(i, i ^ m) for i in range(size)])  99.3 us
    all_to_all x3, blocking collectives, trade(): return lax.all_to_all(value, axes, 0, 0, tiled=True)  90.9 us
    pallas_call x11, Pallas kernels, kernel(): pl.pallas_call(body, out_shape=outs, in_specs=[SMEM()] * scalars + [VMEM(...  34.2 us
    ppermute x9, starting transfers between devices, swap(): return lax.ppermute(value, axis, [(i, i ^ m) for i in range(size)])  30.3 us
    all_to_all x1, starting transfers between devices, trade(): return lax.all_to_all(value, axes, 0, 0, tiled=True)  8.15 us
  transfers between devices with their start and end apart: 10, of which 8 were waited for; matrix products, arithmetic and copies ran while one was open for 0% of the time, Pallas kernels for 4%

profile of v1, /device:TPU:64, one launch (start us, length us, event | category | flops | bytes accessed | tf_op | source)
XLA Modules:
  0.0 271.7 jit_solution(13248644217227733611)
XLA Ops:
  3.6 31.5 %all_to_all.20.got = bf16[8,176,128]{2,1,0:T(8,128)(2,1)} all-to-all(bf16[8,176,128]{2,1,0:T(8,128)(2,1)} %packet.1), channel_id=1, replica_groups=mesh['zh'=2,'y'=4,'c'=2,'zq'=4,'zp'=2,'x'=4] {'zq','zp'}, dimensions={0} | all-to-all | bytes 720896 | tf_op jit(solution)/shard_map/all_to_all | solution.py:272
  35.1 2.5 shard_map.92
  37.6 25.9 %all_to_all.21.own = bf16[16,320,128]{2,1,0:T(8,128)(2,1)S(1)} all-to-all(bf16[16,320,128]{2,1,0:T(8,128)(2,1)} %get-tuple-element.28), channel_id=1, replica_groups=mesh['zh'=2,'y'=4,'c'=2,'zq'=4,'zp'=2,'x'=4] {'y','x'}, dimensions={0} | all-to-all | bytes 2621440 | tf_op jit(solution)/shard_map/all_to_all | solution.py:272
  69.9 5.0 %collective-permute-start.2 = (bf16[512,256]{1,0:T(8,128)(2,1)}, bf16[512,256]{1,0:T(8,128)(2,1)S(1)}, u32[]{:S(2)}, u32[]{:S(2)}) collective-permute-start(bf16[512,256]{1,0:T(8,128)(2,1)} %get-tuple-element.31), channel_id=1, source_target_pairs={{0,16},{8,24},{16,0},{24,8},{1,17},{9,25},{17,1},{25,9},{2,18},{10... | collective-permute-start | bytes 786440 | tf_op jit(solution)/shard_map/ppermute | solution.py:269
  75.0 5.1 %collective-permute-start.3 = (bf16[512,256]{1,0:T(8,128)(2,1)}, bf16[512,256]{1,0:T(8,128)(2,1)S(1)}, u32[]{:S(2)}, u32[]{:S(2)}) collective-permute-start(bf16[512,256]{1,0:T(8,128)(2,1)} %get-tuple-element.32), channel_id=1, source_target_pairs={{0,24},{8,16},{16,8},{24,0},{1,25},{9,17},{17,9},{25,1},{2,26},{10... | collective-permute-start | bytes 786440 | tf_op jit(solution)/shard_map/ppermute | solution.py:269
  80.1 4.3 %collective-permute-done.1.w1 = bf16[512,256]{1,0:T(8,128)(2,1)S(1)} collective-permute-done((bf16[512,256]{1,0:T(8,128)(2,1)}, bf16[512,256]{1,0:T(8,128)(2,1)S(1)}, u32[]{:S(2)}, u32[]{:S(2)}) %collective-permute-start.1) | collective-permute-done | bytes 262176 | tf_op jit(solution)/shard_map/ppermute | solution.py:269
  84.4 24.8 %collective-permute-done.2.w2 = bf16[512,256]{1,0:T(8,128)(2,1)S(1)} collective-permute-done((bf16[512,256]{1,0:T(8,128)(2,1)}, bf16[512,256]{1,0:T(8,128)(2,1)S(1)}, u32[]{:S(2)}, u32[]{:S(2)}) %collective-permute-start.2) | collective-permute-done | bytes 262176 | tf_op jit(solution)/shard_map/ppermute | solution.py:269
  109.2 14.9 %collective-permute-done.3.w3 = bf16[512,256]{1,0:T(8,128)(2,1)S(1)} collective-permute-done((bf16[512,256]{1,0:T(8,128)(2,1)}, bf16[512,256]{1,0:T(8,128)(2,1)S(1)}, u32[]{:S(2)}, u32[]{:S(2)}) %collective-permute-start.3) | collective-permute-done | bytes 262176 | tf_op jit(solution)/shard_map/ppermute | solution.py:269
  125.3 3.6 %shard_map.94.mine = bf16[640,256]{1,0:T(8,128)(2,1)} custom-call(s32[8]{0:T(128)} %stack.26.at, bf16[16,320,128]{2,1,0:T(8,128)(2,1)} %copy-done, bf16[16,320,128]{2,1,0:T(8,128)(2,1)} %copy-done.1, bf16[512,256]{1,0:T(8,128)(2,1)} %get-tuple-element.29.w0, bf16[512,256]{1,0:T(8,128)(2,1)} %copy-done.2, bf16[512,256]{1,0:T(8,128)(2,1)} %copy-done.3, ...), custom_call_target="tpu_custom_call" | custom-call | flops 671088640 | bytes 4194304 | tf_op jit(solution)/shard_map/pallas_call | solution.py:36
  131.4 2.7 %shard_map.95 = (bf16[64,640]{1,0:T(8,128)(2,1)}, bf16[640,128]{1,0:T(8,128)(2,1)}, bf16[1024,640]{1,0:T(8,128)(2,1)}) custom-call(s32[8]{0:T(128)} %stack.26.at, f32[64,128]{1,0:T(8,128)} %get-tuple-element.34.len_ref), custom_call_target="tpu_custom_call" | custom-call | flops 10000000 | bytes 2000000 | tf_op jit(solution)/shard_map/pallas_call | solution.py:36
  134.1 6.4 %collective-permute-done.4.theirs = bf16[640,256]{1,0:T(8,128)(2,1)S(1)} collective-permute-done((bf16[640,256]{1,0:T(8,128)(2,1)}, bf16[640,256]{1,0:T(8,128)(2,1)S(1)}, u32[]{:S(2)}, u32[]{:S(2)}) %collective-permute-start.4) | collective-permute-done | bytes 327712 | tf_op jit(solution)/shard_map/ppermute | solution.py:269
  141.2 3.0 %shard_map.96 = (bf16[640,256]{1,0:T(8,128)(2,1)}, bf16[32,256]{1,0:T(8,128)(2,1)}, bf16[32,256]{1,0:T(8,128)(2,1)}, bf16[32,256]{1,0:T(8,128)(2,1)}, bf16[32,256]{1,0:T(8,128)(2,1)}) custom-call(s32[8]{0:T(128)} %stack.26.at, bf16[640,256]{1,0:T(8,128)(2,1)} %shard_map.94.mine, bf16[640,256]{1,0:T(8,128)(2,1)} %copy-done.7, f32[4,256]{1,0:T(4,128)} %reshape.22.bias, ...), custom_call_target="tpu_custom_call" | custom-call | tf_op jit(solution)/shard_map/pallas_call | solution.py:36
  144.3 4.2 %shard_map.99 = bf16[512,2048]{1,0:T(8,128)(2,1)} custom-call(s32[8]{0:T(128)} %stack.26.at, bf16[1024,640]{1,0:T(8,128)(2,1)} %get-tuple-element.50.spread, bf16[640,256]{1,0:T(8,128)(2,1)} %get-tuple-element.37.grad, bf16[512,256]{1,0:T(8,128)(2,1)} %get-tuple-element.29.w0, bf16[512,256]{1,0:T(8,128)(2,1)} %copy-done.2, bf16[512,256]{1,0:T(8,128)(2,1)} %copy-done.3, ...), custom_call_target="tpu_custom_call" | custom-call | flops 536870912 | bytes 4194304 | tf_op jit(solution)/shard_map/pallas_call | solution.py:36
  150.4 4.3 %collective-permute-done.8.got = bf16[512,2048]{1,0:T(8,128)(2,1)S(1)} collective-permute-done((bf16[512,2048]{1,0:T(8,128)(2,1)}, bf16[512,2048]{1,0:T(8,128)(2,1)S(1)}, u32[]{:S(2)}, u32[]{:S(2)}) %collective-permute-start.8) | collective-permute-done | bytes 2097184 | tf_op jit(solution)/shard_map/ppermute | solution.py:269
  156.1 5.0 %shard_map.100 = bf16[512,2048]{1,0:T(8,128)(2,1)} custom-call(s32[8]{0:T(128)} %stack.26.at, bf16[1024,640]{1,0:T(8,128)(2,1)} %get-tuple-element.50.spread, bf16[640,256]{1,0:T(8,128)(2,1)} %get-tuple-element.37.grad, bf16[512,256]{1,0:T(8,128)(2,1)} %get-tuple-element.29.w0, bf16[512,256]{1,0:T(8,128)(2,1)} %copy-done.2, bf16[512,256]{1,0:T(8,128)(2,1)} %copy-done.3, ...), custom_call_target="tpu_custom_call" | custom-call | flops 536870912 | bytes 6291456 | tf_op jit(solution)/shard_map/pallas_call | solution.py:36
  161.1 33.5 %all_to_all.22.got = bf16[16,32,2048]{2,1,0:T(8,128)(2,1)} all-to-all(bf16[16,32,2048]{2,1,0:T(8,128)(2,1)} %bitcast.8), channel_id=1, replica_groups=mesh['zh'=2,'y'=4,'c'=2,'zq'=4,'zp'=2,'x'=4] {'y','x'}, dimensions={0} | all-to-all | bytes 4194304 | tf_op jit(solution)/shard_map/all_to_all | solution.py:272
  194.6 2.5 shard_map.101
  197.2 8.1 %all-to-all-start.3 = ((bf16[8,16,512]{2,1,0:T(8,128)(2,1)}), bf16[8,16,512]{2,1,0:T(8,128)(2,1)S(1)}, u32[]{:S(2)}, u32[]{:S(2)}) async-start(bf16[8,16,512]{2,1,0:T(8,128)(2,1)} %shard_map.101), calls=%async_computation.3 | async-start | bytes 262144 | tf_op jit(solution)/shard_map/all_to_all | solution.py:272
  205.3 4.0 %shard_map.97 = (bf16[544,256]{1,0:T(8,128)(2,1)}, bf16[544,256]{1,0:T(8,128)(2,1)}, bf16[544,256]{1,0:T(8,128)(2,1)}, bf16[544,256]{1,0:T(8,128)(2,1)}) custom-call(s32[8]{0:T(128)} %stack.26.at, bf16[16,320,128]{2,1,0:T(8,128)(2,1)} %copy-done, bf16[16,320,128]{2,1,0:T(8,128)(2,1)} %copy-done.1, bf16[640,256]{1,0:T(8,128)(2,1)} %get-tuple-element.37.grad, ...), custom_call_target="tpu_custom_call" | custom-call | flops 671088640 | bytes 4194304 | tf_op jit(solution)/shard_map/pallas_call | solution.py:36
  211.3 7.8 %collective-permute-start.6 = (bf16[544,256]{1,0:T(8,128)(2,1)}, bf16[544,256]{1,0:T(8,128)(2,1)S(1)}, u32[]{:S(2)}, u32[]{:S(2)}) collective-permute-start(bf16[544,256]{1,0:T(8,128)(2,1)} %get-tuple-element.44), channel_id=1, source_target_pairs={{0,16},{8,24},{16,0},{24,8},{1,17},{9,25},{17,1},{25,9},{2,18},{10... | collective-permute-start | bytes 835592 | tf_op jit(solution)/shard_map/ppermute | solution.py:269
  221.6 8.5 %collective-permute-done.5.p1 = bf16[544,256]{1,0:T(8,128)(2,1)S(1)} collective-permute-done((bf16[544,256]{1,0:T(8,128)(2,1)}, bf16[544,256]{1,0:T(8,128)(2,1)S(1)}, u32[]{:S(2)}, u32[]{:S(2)}) %collective-permute-start.5) | collective-permute-done | bytes 278560 | tf_op jit(solution)/shard_map/ppermute | solution.py:269
  230.1 23.8 %collective-permute-done.6.p2 = bf16[544,256]{1,0:T(8,128)(2,1)S(1)} collective-permute-done((bf16[544,256]{1,0:T(8,128)(2,1)}, bf16[544,256]{1,0:T(8,128)(2,1)S(1)}, u32[]{:S(2)}, u32[]{:S(2)}) %collective-permute-start.6) | collective-permute-done | bytes 278560 | tf_op jit(solution)/shard_map/ppermute | solution.py:269
  253.9 12.2 %collective-permute-done.7.p3 = bf16[544,256]{1,0:T(8,128)(2,1)S(1)} collective-permute-done((bf16[544,256]{1,0:T(8,128)(2,1)}, bf16[544,256]{1,0:T(8,128)(2,1)S(1)}, u32[]{:S(2)}, u32[]{:S(2)}) %collective-permute-start.7) | collective-permute-done | bytes 278560 | tf_op jit(solution)/shard_map/ppermute | solution.py:269
  266.8 2.7 shard_map.98
  (37 shorter events, 24.3 us)
Async XLA Ops:
  63.5 60.7 %copy-start = (bf16[16,320,128]{2,1,0:T(8,128)(2,1)}, bf16[16,320,128]{2,1,0:T(8,128)(2,1)S(1)}, u32[]{:S(2)}) copy-start(bf16[16,320,128]{2,1,0:T(8,128)(2,1)S(1)} %all_to_all.21.own) | copy-start | bytes 3932164
  63.5 60.7 %collective-permute-start = (bf16[16,320,128]{2,1,0:T(8,128)(2,1)S(1)}, bf16[16,320,128]{2,1,0:T(8,128)(2,1)S(1)}, u32[]{:S(2)}, u32[]{:S(2)}) collective-permute-start(bf16[16,320,128]{2,1,0:T(8,128)(2,1)S(1)} %all_to_all.21.own), channel_id=1, source_target_pairs={{0,32},{32,0},{1,33},{33,1},{2,34},{34,2},{3,35},{35,3},{4,36},{36... | collective-permute-start | bytes 3932168 | tf_op jit(solution)/shard_map/ppermute | solution.py:269
  67.7 63.0 %copy-start.11 = (f32[1024]{0:T(1024)S(1)}, f32[1024]{0:T(1024)}, u32[]{:S(2)}) copy-start(f32[1024]{0:T(1024)} %param.7) | copy-start | bytes 12292
  67.7 16.6 %collective-permute-start.1 = (bf16[512,256]{1,0:T(8,128)(2,1)}, bf16[512,256]{1,0:T(8,128)(2,1)S(1)}, u32[]{:S(2)}, u32[]{:S(2)}) collective-permute-start(bf16[512,256]{1,0:T(8,128)(2,1)} %get-tuple-element.30), channel_id=1, source_target_pairs={{0,8},{8,0},{16,24},{24,16},{1,9},{9,1},{17,25},{25,17},{2,10},{10... | collective-permute-start | bytes 786440 | tf_op jit(solution)/shard_map/ppermute | solution.py:269
  69.9 39.2 %collective-permute-start.2 = (bf16[512,256]{1,0:T(8,128)(2,1)}, bf16[512,256]{1,0:T(8,128)(2,1)S(1)}, u32[]{:S(2)}, u32[]{:S(2)}) collective-permute-start(bf16[512,256]{1,0:T(8,128)(2,1)} %get-tuple-element.31), channel_id=1, source_target_pairs={{0,16},{8,24},{16,0},{24,8},{1,17},{9,25},{17,1},{25,9},{2,18},{10... | collective-permute-start | bytes 786440 | tf_op jit(solution)/shard_map/ppermute | solution.py:269
  75.0 49.1 %collective-permute-start.3 = (bf16[512,256]{1,0:T(8,128)(2,1)}, bf16[512,256]{1,0:T(8,128)(2,1)S(1)}, u32[]{:S(2)}, u32[]{:S(2)}) collective-permute-start(bf16[512,256]{1,0:T(8,128)(2,1)} %get-tuple-element.32), channel_id=1, source_target_pairs={{0,24},{8,16},{16,8},{24,0},{1,25},{9,17},{17,9},{25,1},{2,26},{10... | collective-permute-start | bytes 786440 | tf_op jit(solution)/shard_map/ppermute | solution.py:269
  84.4 39.8 %copy-start.2 = (bf16[512,256]{1,0:T(8,128)(2,1)}, bf16[512,256]{1,0:T(8,128)(2,1)S(1)}, u32[]{:S(2)}) copy-start(bf16[512,256]{1,0:T(8,128)(2,1)S(1)} %collective-permute-done.1.w1) | copy-start | bytes 786436
  109.2 15.0 %copy-start.3 = (bf16[512,256]{1,0:T(8,128)(2,1)}, bf16[512,256]{1,0:T(8,128)(2,1)S(1)}, u32[]{:S(2)}) copy-start(bf16[512,256]{1,0:T(8,128)(2,1)S(1)} %collective-permute-done.2.w2) | copy-start | bytes 786436
  124.1 0.7 copy-start.4
  124.1 1.2 copy-start.1
  128.8 11.7 %collective-permute-start.4 = (bf16[640,256]{1,0:T(8,128)(2,1)}, bf16[640,256]{1,0:T(8,128)(2,1)S(1)}, u32[]{:S(2)}, u32[]{:S(2)}) collective-permute-start(bf16[640,256]{1,0:T(8,128)(2,1)} %shard_map.94.mine), channel_id=1, source_target_pairs={{0,4},{4,0},{1,5},{5,1},{2,6},{6,2},{3,7},{7,3},{8,12},{12,8},{9,1... | collective-permute-start | bytes 983048 | tf_op jit(solution)/shard_map/ppermute | solution.py:269
  140.5 0.7 copy-start.7
  148.5 6.3 %collective-permute-start.8 = (bf16[512,2048]{1,0:T(8,128)(2,1)}, bf16[512,2048]{1,0:T(8,128)(2,1)S(1)}, u32[]{:S(2)}, u32[]{:S(2)}) collective-permute-start(bf16[512,2048]{1,0:T(8,128)(2,1)} %shard_map.99), channel_id=1, source_target_pairs={{0,32},{32,0},{1,33},{33,1},{2,34},{34,2},{3,35},{35,3},{4,36},{36... | collective-permute-start | bytes 6291464 | tf_op jit(solution)/shard_map/ppermute | solution.py:269
  154.8 1.3 copy-start.5
  197.2 72.3 %all-to-all-start.3 = ((bf16[8,16,512]{2,1,0:T(8,128)(2,1)}), bf16[8,16,512]{2,1,0:T(8,128)(2,1)S(1)}, u32[]{:S(2)}, u32[]{:S(2)}) async-start(bf16[8,16,512]{2,1,0:T(8,128)(2,1)} %shard_map.101), calls=%async_computation.3 | async-start | bytes 262144 | tf_op jit(solution)/shard_map/all_to_all | solution.py:272
  209.3 20.8 %collective-permute-start.5 = (bf16[544,256]{1,0:T(8,128)(2,1)}, bf16[544,256]{1,0:T(8,128)(2,1)S(1)}, u32[]{:S(2)}, u32[]{:S(2)}) collective-permute-start(bf16[544,256]{1,0:T(8,128)(2,1)} %get-tuple-element.43), channel_id=1, source_target_pairs={{0,8},{8,0},{16,24},{24,16},{1,9},{9,1},{17,25},{25,17},{2,10},{10... | collective-permute-start | bytes 835592 | tf_op jit(solution)/shard_map/ppermute | solution.py:269
  211.3 42.7 %collective-permute-start.6 = (bf16[544,256]{1,0:T(8,128)(2,1)}, bf16[544,256]{1,0:T(8,128)(2,1)S(1)}, u32[]{:S(2)}, u32[]{:S(2)}) collective-permute-start(bf16[544,256]{1,0:T(8,128)(2,1)} %get-tuple-element.44), channel_id=1, source_target_pairs={{0,16},{8,24},{16,0},{24,8},{1,17},{9,25},{17,1},{25,9},{2,18},{10... | collective-permute-start | bytes 835592 | tf_op jit(solution)/shard_map/ppermute | solution.py:269
  219.1 47.0 %collective-permute-start.7 = (bf16[544,256]{1,0:T(8,128)(2,1)}, bf16[544,256]{1,0:T(8,128)(2,1)S(1)}, u32[]{:S(2)}, u32[]{:S(2)}) collective-permute-start(bf16[544,256]{1,0:T(8,128)(2,1)} %get-tuple-element.45), channel_id=1, source_target_pairs={{0,24},{8,16},{16,8},{24,0},{1,25},{9,17},{17,9},{25,1},{2,26},{10... | collective-permute-start | bytes 835592 | tf_op jit(solution)/shard_map/ppermute | solution.py:269
  230.1 36.0 %copy-start.8 = (bf16[544,256]{1,0:T(8,128)(2,1)}, bf16[544,256]{1,0:T(8,128)(2,1)S(1)}, u32[]{:S(2)}) copy-start(bf16[544,256]{1,0:T(8,128)(2,1)S(1)} %collective-permute-done.5.p1) | copy-start | bytes 835588
  253.9 12.2 %copy-start.9 = (bf16[544,256]{1,0:T(8,128)(2,1)}, bf16[544,256]{1,0:T(8,128)(2,1)S(1)}, u32[]{:S(2)}) copy-start(bf16[544,256]{1,0:T(8,128)(2,1)S(1)} %collective-permute-done.6.p2) | copy-start | bytes 835588
  266.1 0.7 copy-start.10
  269.5 0.7 copy-start.6

commit v2 on v1

--- a/solution.py
+++ b/solution.py
@@ -28,18 +28,27 @@
 SMEM = functools.partial(pl.BlockSpec, memory_space=pltpu.SMEM)
 
 
-def call(body, outs, ins, flops=0, moved=0, scalars=1):
-    return kernel(body, outs, ins, flops, moved, scalars)
-
-
-def kernel(body, outs, ins, flops, moved, scalars):
+def call(body, outs, ins, flops=0, moved=0, name=None):
+    return kernel(body, outs, ins, flops, moved, name)
+
+
+def kernel(body, outs, ins, flops, moved, name):
+    ins = [pltpu.with_memory_space_constraint(x, pltpu.VMEM) for x in ins]
     return pl.pallas_call(
         body,
-        out_shape=outs,
-        in_specs=[SMEM()] * scalars + [VMEM()] * (len(ins) - scalars),
+        out_shape=jax.tree.map(lambda o: pltpu.VMEM(o.shape, o.dtype), outs) if name in KEEP else outs,
+        in_specs=[VMEM()] * len(ins),
         out_specs=jax.tree.map(lambda _: VMEM(), outs),
+        compiler_params=pltpu.CompilerParams(vmem_limit_bytes=20 << 20),
         cost_estimate=pl.CostEstimate(flops=flops, bytes_accessed=moved, transcendentals=0),
     )(*ins)
+
+
+KEEP = ("weights", "compact", "logits", "grads", "send", "keep", "plane", "weight_grad", "tables")
+
+
+def home():
+    return lax.axis_index("zq"), lax.axis_index("zp"), lax.axis_index("c")
 
 
 def iota(shape, dim):
@@ -55,13 +64,28 @@
     return lax.dot_general(left, right, (dims, ((), ())), preferred_element_type=F32)
 
 
-def weights_body(at, w_ref, *outs):
-    for m, out in enumerate(outs):
+def weights_body(w_ref, o0, o1, o2, o3, sems):
+    at = home()
+    copies = []
+    for m, out in enumerate((o0, o1, o2, o3)):
         start = pl.multiple_of((at[0] ^ m) * CUT, CUT)
-        out[...] = w_ref[:, pl.ds(start, CUT)]
-
-
-def packet_body(at, lengths, even_ref, odd_ref, cot_ref, out):
+        copies.append(pltpu.make_async_copy(w_ref.at[:, pl.ds(start, CUT)], out, sems.at[m]))
+        copies[-1].start()
+    for copy in copies:
+        copy.wait()
+
+
+def packet_body(lengths, hidden_ref, cot_hbm, out, even_ref, odd_ref, cot_ref, sems):
+    spot = (8 * lax.axis_index("y") + lax.axis_index("x")) * LANES
+    copies = []
+    for i, ref in enumerate((even_ref, odd_ref)):
+        start = pl.multiple_of(spot + i * BLOCK, LANES)
+        copies.append(pltpu.make_async_copy(hidden_ref.at[:, pl.ds(start, LANES)], ref, sems.at[i]))
+    copies.append(pltpu.make_async_copy(cot_hbm, cot_ref, sems.at[2]))
+    for copy in copies:
+        copy.start()
+    for copy in copies:
+        copy.wait()
     row = iota((16, LANES), 0)
     lens = jnp.zeros((16, LANES), F32)
     for s in range(8):
@@ -80,7 +104,8 @@
             out[k, 160:176, :] = pieces[1]
 
 
-def compact_body(at, got, out, cot_out, len_out):
+def compact_body(got, out, cot_out, len_out):
+    at = home()
     column = jnp.concatenate([got[k, 128:144, :].astype(F32)[0:8] for k in range(8)], axis=0)
     len_out[...] = column
     wide = jnp.broadcast_to(column[:, 0:1], (SEQS, TOKENS))
@@ -104,7 +129,8 @@
         cot_out[k * 8 : (k + 1) * 8, LANES:CUT] = both[8:16]
 
 
-def tables_body(at, len_ref, seg_ref, segt_ref, spread_ref):
+def tables_body(len_ref, seg_ref, segt_ref, spread_ref):
+    at = home()
     lens = len_ref[...]
     sub = iota((SEQS, LANES), 0)
     lane = iota((SEQS, LANES), 1)
@@ -139,7 +165,8 @@
     return jnp.concatenate([ref[block * 4 + i] for i in range(4)], axis=1)
 
 
-def logits_body(at, own, other, w0, w1, w2, w3, out):
+def logits_body(own, other, w0, w1, w2, w3, out):
+    at = home()
     for hop, ref in enumerate((own, other)):
         total = jnp.zeros((HALF, CUT), F32)
         for m, w in enumerate((w0, w1, w2, w3)):
@@ -148,7 +175,8 @@
         out[pl.ds(pl.multiple_of(half * HALF, HALF), HALF), :] = total.astype(BF16)
 
 
-def grads_body(at, mine, theirs, bias, cot, seg, segt, grad_out, x0, x1, x2, x3):
+def grads_body(mine, theirs, bias, cot, seg, segt, grad_out, x0, x1, x2, x3):
+    at = home()
     logits = mine[...].astype(F32) + theirs[...].astype(F32) + bias[pl.ds(at[0], 1), :]
     positive = jnp.maximum(logits, 0.0)
     act = jnp.log1p(positive)
@@ -184,7 +212,8 @@
         out[16:32, :] = tail
 
 
-def weight_grad_body(at, own, other, grad, x0, x1, x2, x3, o0, o1, o2, o3):
+def weight_grad_body(own, other, grad, x0, x1, x2, x3, o0, o1, o2, o3):
+    at = home()
     for m, (extra, out) in enumerate(zip((x0, x1, x2, x3), (o0, o1, o2, o3))):
         total = jnp.zeros((BLOCK, CUT), F32)
         for hop, ref in enumerate((own, other)):
@@ -195,14 +224,16 @@
         out[BLOCK : BLOCK + EXTRA, :] = extra[...]
 
 
-def send_body(at, spread, grad, w0, w1, w2, w3, out):
+def send_body(spread, grad, w0, w1, w2, w3, out):
+    at = home()
     rows = dot(spread[TOKENS // 2 :, :], grad[...]).astype(BF16)
     for m, w in enumerate((w0, w1, w2, w3)):
         start = pl.multiple_of((at[0] ^ m) * BLOCK, BLOCK)
         out[:, pl.ds(start, BLOCK)] = dot(rows, w[...], ((1,), (1,))).astype(BF16)
 
 
-def keep_body(at, spread, grad, w0, w1, w2, w3, got, out):
+def keep_body(spread, grad, w0, w1, w2, w3, got, out):
+    at = home()
     rows = dot(spread[: TOKENS // 2, :], grad[...]).astype(BF16)
     for m, w in enumerate((w0, w1, w2, w3)):
         start = pl.multiple_of((at[0] ^ m) * BLOCK, BLOCK)
@@ -227,7 +258,8 @@
     out[...] = total
 
 
-def unpack_body(at, p0, p1, p2, p3, weight_out, pooled_out, mean_out, bias_out):
+def unpack_body(p0, p1, p2, p3, weight_out, pooled_out, mean_out, bias_out):
+    at = home()
     for m, piece in enumerate((p0, p1, p2, p3)):
         columns = pl.ds(pl.multiple_of((at[0] ^ m) * CUT, CUT), CUT)
         weight_out[:, columns] = piece[0:BLOCK, :].astype(F32)
@@ -237,22 +269,33 @@
         bias_out[:, columns] = extra[18:19] + extra[19:20]
 
 
-def pack(at, lengths, hidden, rep_cotangent):
+def pack(lengths, hidden, rep_cotangent):
     return pl.pallas_call(
         packet_body,
-        grid_spec=pltpu.PrefetchScalarGridSpec(
-            num_scalar_prefetch=2,
-            grid=(1,),
-            in_specs=[
-                pl.BlockSpec((128, LANES), lambda i, at, n: (0, at[4])),
-                pl.BlockSpec((128, LANES), lambda i, at, n: (0, at[4] + 4)),
-                pl.BlockSpec((8, 1024), lambda i, at, n: (0, 0)),
-            ],
-            out_specs=pl.BlockSpec((8, PACK, LANES), lambda i, at, n: (0, 0, 0)),
-        ),
-        out_shape=shape((8, PACK, LANES)),
+        out_shape=pltpu.VMEM((8, PACK, LANES), BF16),
+        in_specs=[SMEM(), pl.BlockSpec(memory_space=pltpu.HBM), pl.BlockSpec(memory_space=pltpu.HBM)],
+        out_specs=VMEM(),
+        scratch_shapes=[
+            pltpu.VMEM((128, LANES), BF16),
+            pltpu.VMEM((128, LANES), BF16),
+            pltpu.VMEM((8, 1024), F32),
+            pltpu.SemaphoreType.DMA((3,)),
+        ],
+        compiler_params=pltpu.CompilerParams(vmem_limit_bytes=8 << 20),
         name="packet",
-    )(at, lengths, hidden, hidden, rep_cotangent)
+    )(lengths, hidden, rep_cotangent)
+
+
+def cut(head_weight):
+    return pl.pallas_call(
+        weights_body,
+        out_shape=[pltpu.VMEM((BLOCK, CUT), BF16)] * 4,
+        in_specs=[pl.BlockSpec(memory_space=pltpu.HBM)],
+        out_specs=[VMEM()] * 4,
+        scratch_shapes=[pltpu.SemaphoreType.DMA((4,))],
+        compiler_params=pltpu.CompilerParams(vmem_limit_bytes=8 << 20),
+        name="weights",
+    )(head_weight)
 
 
 def shape(dims, kind=BF16):
@@ -260,68 +303,68 @@
 
 
 def per_device(hidden, head_weight, head_bias, rep_cotangent, lengths):
-    a, q, c = lax.axis_index("zq"), lax.axis_index("zp"), lax.axis_index("c")
-    j = lax.axis_index("y") * 4 + lax.axis_index("x")
-    spot = (2 * (j // 4)) * 4 + j % 4
-    at = jnp.stack([a, q, c, j, spot, spot, spot, spot]).astype(I32)
-
     def swap(value, axis, size, m):
         return lax.ppermute(value, axis, [(i, i ^ m) for i in range(size)])
 
     def trade(value, axes):
         return lax.all_to_all(value, axes, 0, 0, tiled=True)
 
-    w = call(weights_body, [shape((BLOCK, CUT))] * 4, [at, head_weight])
+    w = cut(head_weight)
     w = [w[0]] + [swap(w[m], "zq", 4, m) for m in (1, 2, 3)]
 
-    packets = pack(at, lengths, hidden, rep_cotangent)
+    packets = pack(lengths, hidden, rep_cotangent)
     got = trade(packets, ("zq", "zp"))
     rows, cot, lens = call(
         compact_body,
         [shape((16, HALF, LANES)), shape((SEQS, CUT), F32), shape((SEQS, LANES), F32)],
-        [at, got],
+        [got],
+        name="compact",
     )
     own = trade(rows, ("y", "x"))
     other = swap(own, "c", 2, 1)
     seg, segt, spread = call(
         tables_body,
         [shape((SEQS, LIVE)), shape((LIVE, LANES)), shape((TOKENS, LIVE))],
-        [at, lens],
+        [lens],
         flops=10_000_000,
         moved=2_000_000,
+        name="tables",
     )
     mine = call(
-        logits_body, shape((LIVE, CUT)), [at, own, other, *w], 2 * LIVE * 2048 * CUT, 4 << 20
+        logits_body, shape((LIVE, CUT)), [own, other, *w], 2 * LIVE * 2048 * CUT, 4 << 20, name="logits"
     )
     theirs = swap(mine, "zp", 2, 1)
     grad, *extra = call(
         grads_body,
         [shape((LIVE, CUT))] + [shape((EXTRA, CUT))] * 4,
-        [at, mine, theirs, head_bias.reshape(4, CUT), cot, seg, segt],
+        [mine, theirs, head_bias.reshape(4, CUT), cot, seg, segt],
+        name="grads",
     )
     send = call(
-        send_body, shape((512, 2048)), [at, spread, grad, *w], 2 * 512 * 2048 * CUT, 4 << 20
+        send_body, shape((512, 2048)), [spread, grad, *w], 2 * 512 * 2048 * CUT, 4 << 20, name="send"
     )
     came = swap(send, "c", 2, 1)
     pieces = call(
         weight_grad_body,
         [shape((BLOCK + EXTRA, CUT))] * 4,
-        [at, own, other, grad, *extra],
+        [own, other, grad, *extra],
         2 * LIVE * 2048 * CUT,
         4 << 20,
+        name="weight_grad",
     )
     pieces = [pieces[0]] + [swap(pieces[m], "zq", 4, m) for m in (1, 2, 3)]
     kept = call(
-        keep_body, shape((512, 2048)), [at, spread, grad, *w, came], 2 * 512 * 2048 * CUT, 6 << 20
+        keep_body, shape((512, 2048)), [spread, grad, *w, came], 2 * 512 * 2048 * CUT, 6 << 20, name="keep"
     )
     plane = trade(kept.reshape(16, 32, 2048), ("y", "x"))
-    column = call(plane_body, shape((8, 16, BLOCK)), [plane], scalars=0)
+    column = call(plane_body, shape((8, 16, BLOCK)), [plane], name="plane")
     column = trade(column, ("zh", "zq"))
-    input_grad = call(last_body, shape((16, BLOCK), F32), [column], scalars=0)
+    input_grad = call(last_body, shape((16, BLOCK), F32), [column], name="last")
     weight_grad, pooled, mean, bias_grad = call(
         unpack_body,
         [shape((BLOCK, 1024), F32), shape((8, 1024), F32), shape((1, 1024), F32), shape((1, 1024), F32)],
-        [at, *pieces],
+        [*pieces],
+        name="unpack",
     )
     return pooled, mean.reshape(1024), bias_grad.reshape(1024), weight_grad, input_grad
 

time: 273 us -> 251 us (0.919)
  Pallas kernels: 36.5 us -> 12.8 us
    pallas_call x12, Pallas kernels: 36.5 us -> 12.8 us  [the longest x10 11.9 us: kernel(): pl.pallas_call(body, out_shape=jax.tree.map(lambda o: pltpu.VMEM(o.shape,...]
    unnamed x24 -> x34, local copies, waits for them, and re-layouts: 4.55 us -> 7.75 us
  transfers between devices with their start and end apart: 10 -> 10, of which waited for: 8 -> 8; matrix products, arithmetic and copies ran while one was open for 0% -> 0% of each run, Pallas kernels for 4% -> 2%
where the time goes in v2:
time: 251 us
  waiting for transfers between devices  102 us (41%)
  blocking collectives  88.7 us (35%)
  starting transfers between devices  38.3 us (15%)
  Pallas kernels  12.8 us (5%)
  local copies, waits for them, and re-layouts  8.35 us (3%)
    ppermute x9, waiting for transfers between devices, swap(): return lax.ppermute(value, axis, [(i, i ^ m) for i in range(size)])  102 us
    all_to_all x3, blocking collectives, trade(): return lax.all_to_all(value, axes, 0, 0, tiled=True)  88.7 us
    ppermute x9, starting transfers between devices, swap(): return lax.ppermute(value, axis, [(i, i ^ m) for i in range(size)])  30.2 us
    pallas_call x10, Pallas kernels, kernel(): pl.pallas_call(body, out_shape=jax.tree.map(lambda o: pltpu.VMEM(o.shape,...  11.9 us
    all_to_all x1, starting transfers between devices, trade(): return lax.all_to_all(value, axes, 0, 0, tiled=True)  8.15 us
    unnamed x34, local copies, waits for them, and re-layouts  7.75 us
  transfers between devices with their start and end apart: 10, of which 8 were waited for; matrix products, arithmetic and copies ran while one was open for 0% of the time, Pallas kernels for 2%

profile of v2, /device:TPU:64, one launch (start us, length us, event | category | flops | bytes accessed | tf_op | source)
XLA Modules:
  0.0 250.6 jit_solution(8934562628496655050)
XLA Ops:
  4.0 31.3 %all_to_all.20.got = bf16[8,176,128]{2,1,0:T(8,128)(2,1)S(1)} all-to-all(bf16[8,176,128]{2,1,0:T(8,128)(2,1)S(1)} %packet.1), channel_id=1, replica_groups=mesh['zh'=2,'y'=4,'c'=2,'zq'=4,'zp'=2,'x'=4] {'zq','zp'}, dimensions={0} | all-to-all | bytes 720896 | tf_op jit(solution)/shard_map/all_to_all | solution.py:310
  35.8 25.7 %all_to_all.21.own = bf16[16,320,128]{2,1,0:T(8,128)(2,1)S(1)} all-to-all(bf16[16,320,128]{2,1,0:T(8,128)(2,1)S(1)} %get-tuple-element.28), channel_id=1, replica_groups=mesh['zh'=2,'y'=4,'c'=2,'zq'=4,'zp'=2,'x'=4] {'y','x'}, dimensions={0} | all-to-all | bytes 2621440 | tf_op jit(solution)/shard_map/all_to_all | solution.py:310
  61.4 1.9 collective-permute-start
  63.6 2.1 collective-permute-start.1
  65.7 5.0 %collective-permute-start.2 = (bf16[512,256]{1,0:T(8,128)(2,1)S(1)}, bf16[512,256]{1,0:T(8,128)(2,1)S(1)}, u32[]{:S(2)}, u32[]{:S(2)}) collective-permute-start(bf16[512,256]{1,0:T(8,128)(2,1)S(1)} %get-tuple-element.31), channel_id=1, source_target_pairs={{0,16},{8,24},{16,0},{24,8},{1,17},{9,25},{17,1},{25,9},{2,18},{10... | collective-permute-start | bytes 786440 | tf_op jit(solution)/shard_map/ppermute | solution.py:307
  70.7 5.1 %collective-permute-start.3 = (bf16[512,256]{1,0:T(8,128)(2,1)S(1)}, bf16[512,256]{1,0:T(8,128)(2,1)S(1)}, u32[]{:S(2)}, u32[]{:S(2)}) collective-permute-start(bf16[512,256]{1,0:T(8,128)(2,1)S(1)} %get-tuple-element.32), channel_id=1, source_target_pairs={{0,24},{8,16},{16,8},{24,0},{1,25},{9,17},{17,9},{25,1},{2,26},{10... | collective-permute-start | bytes 786440 | tf_op jit(solution)/shard_map/ppermute | solution.py:307
  75.8 4.0 %collective-permute-done.1.w1 = bf16[512,256]{1,0:T(8,128)(2,1)S(1)} collective-permute-done((bf16[512,256]{1,0:T(8,128)(2,1)S(1)}, bf16[512,256]{1,0:T(8,128)(2,1)S(1)}, u32[]{:S(2)}, u32[]{:S(2)}) %collective-permute-start.1) | collective-permute-done | bytes 262176 | tf_op jit(solution)/shard_map/ppermute | solution.py:307
  79.8 24.8 %collective-permute-done.2.w2 = bf16[512,256]{1,0:T(8,128)(2,1)S(1)} collective-permute-done((bf16[512,256]{1,0:T(8,128)(2,1)S(1)}, bf16[512,256]{1,0:T(8,128)(2,1)S(1)}, u32[]{:S(2)}, u32[]{:S(2)}) %collective-permute-start.2) | collective-permute-done | bytes 262176 | tf_op jit(solution)/shard_map/ppermute | solution.py:307
  104.6 15.0 %collective-permute-done.3.w3 = bf16[512,256]{1,0:T(8,128)(2,1)S(1)} collective-permute-done((bf16[512,256]{1,0:T(8,128)(2,1)S(1)}, bf16[512,256]{1,0:T(8,128)(2,1)S(1)}, u32[]{:S(2)}, u32[]{:S(2)}) %collective-permute-start.3) | collective-permute-done | bytes 262176 | tf_op jit(solution)/shard_map/ppermute | solution.py:307
  119.7 1.6 shard_map.93.mine
  121.9 1.9 collective-permute-start.4
  125.3 8.4 %collective-permute-done.4.theirs = bf16[640,256]{1,0:T(8,128)(2,1)} collective-permute-done((bf16[640,256]{1,0:T(8,128)(2,1)}, bf16[640,256]{1,0:T(8,128)(2,1)}, u32[]{:S(2)}, u32[]{:S(2)}) %collective-permute-start.4) | collective-permute-done | bytes 327712 | tf_op jit(solution)/shard_map/ppermute | solution.py:307
  134.4 2.2 shard_map.95
  141.6 1.9 collective-permute-start.8
  143.5 4.1 %collective-permute-done.8.got = bf16[512,2048]{1,0:T(8,128)(2,1)S(1)} collective-permute-done((bf16[512,2048]{1,0:T(8,128)(2,1)S(1)}, bf16[512,2048]{1,0:T(8,128)(2,1)S(1)}, u32[]{:S(2)}, u32[]{:S(2)}) %collective-permute-start.8) | collective-permute-done | bytes 2097184 | tf_op jit(solution)/shard_map/ppermute | solution.py:307
  148.9 31.7 %all_to_all.22.got = bf16[16,32,2048]{2,1,0:T(8,128)(2,1)S(1)} all-to-all(bf16[16,32,2048]{2,1,0:T(8,128)(2,1)S(1)} %bitcast.3), channel_id=1, replica_groups=mesh['zh'=2,'y'=4,'c'=2,'zq'=4,'zp'=2,'x'=4] {'y','x'}, dimensions={0} | all-to-all | bytes 4194304 | tf_op jit(solution)/shard_map/all_to_all | solution.py:310
  181.5 8.1 %all-to-all-start.3 = ((bf16[8,16,512]{2,1,0:T(8,128)(2,1)}), bf16[8,16,512]{2,1,0:T(8,128)(2,1)S(1)}, u32[]{:S(2)}, u32[]{:S(2)}) async-start(bf16[8,16,512]{2,1,0:T(8,128)(2,1)} %shard_map.100), calls=%async_computation.3 | async-start | bytes 262144 | tf_op jit(solution)/shard_map/all_to_all | solution.py:310
  191.0 1.9 collective-permute-start.5
  193.0 7.8 %collective-permute-start.6 = (bf16[544,256]{1,0:T(8,128)(2,1)S(1)}, bf16[544,256]{1,0:T(8,128)(2,1)S(1)}, u32[]{:S(2)}, u32[]{:S(2)}) collective-permute-start(bf16[544,256]{1,0:T(8,128)(2,1)S(1)} %get-tuple-element.44), channel_id=1, source_target_pairs={{0,16},{8,24},{16,0},{24,8},{1,17},{9,25},{17,1},{25,9},{2,18},{10... | collective-permute-start | bytes 835592 | tf_op jit(solution)/shard_map/ppermute | solution.py:307
  200.8 2.5 collective-permute-start.7
  203.3 20.8 %collective-permute-done.5.p1 = bf16[544,256]{1,0:T(8,128)(2,1)S(1)} collective-permute-done((bf16[544,256]{1,0:T(8,128)(2,1)S(1)}, bf16[544,256]{1,0:T(8,128)(2,1)S(1)}, u32[]{:S(2)}, u32[]{:S(2)}) %collective-permute-start.5) | collective-permute-done | bytes 278560 | tf_op jit(solution)/shard_map/ppermute | solution.py:307
  224.0 11.9 %collective-permute-done.6.p2 = bf16[544,256]{1,0:T(8,128)(2,1)S(1)} collective-permute-done((bf16[544,256]{1,0:T(8,128)(2,1)S(1)}, bf16[544,256]{1,0:T(8,128)(2,1)S(1)}, u32[]{:S(2)}, u32[]{:S(2)}) %collective-permute-start.6) | collective-permute-done | bytes 278560 | tf_op jit(solution)/shard_map/ppermute | solution.py:307
  236.0 12.5 %collective-permute-done.7.p3 = bf16[544,256]{1,0:T(8,128)(2,1)S(1)} collective-permute-done((bf16[544,256]{1,0:T(8,128)(2,1)S(1)}, bf16[544,256]{1,0:T(8,128)(2,1)S(1)}, u32[]{:S(2)}, u32[]{:S(2)}) %collective-permute-start.7) | collective-permute-done | bytes 278560 | tf_op jit(solution)/shard_map/ppermute | solution.py:307
  248.4 1.5 shard_map.97
  (46 shorter events, 15.9 us)
Async XLA Ops:
  0.6 1.2 copy-start.5
  1.9 0.8 copy-start.7
  2.6 0.7 copy-start.15
  4.0 59.4 %copy-start.6 = (bf16[512,1024]{1,0:T(8,128)(2,1)S(1)}, bf16[512,1024]{1,0:T(8,128)(2,1)}, u32[]{:S(2)}) copy-start(bf16[512,1024]{1,0:T(8,128)(2,1)} %w_ref.1) | copy-start | bytes 3145732
  61.4 58.2 %collective-permute-start = (bf16[16,320,128]{2,1,0:T(8,128)(2,1)S(1)}, bf16[16,320,128]{2,1,0:T(8,128)(2,1)S(1)}, u32[]{:S(2)}, u32[]{:S(2)}) collective-permute-start(bf16[16,320,128]{2,1,0:T(8,128)(2,1)S(1)} %all_to_all.21.own), channel_id=1, source_target_pairs={{0,32},{32,0},{1,33},{33,1},{2,34},{34,2},{3,35},{35,3},{4,36},{36... | collective-permute-start | bytes 3932168 | tf_op jit(solution)/shard_map/ppermute | solution.py:307
  63.6 60.3 %copy-start.16 = (f32[1024]{0:T(1024)S(1)}, f32[1024]{0:T(1024)}, u32[]{:S(2)}) copy-start(f32[1024]{0:T(1024)} %param.7) | copy-start | bytes 12292
  63.6 16.2 %collective-permute-start.1 = (bf16[512,256]{1,0:T(8,128)(2,1)S(1)}, bf16[512,256]{1,0:T(8,128)(2,1)S(1)}, u32[]{:S(2)}, u32[]{:S(2)}) collective-permute-start(bf16[512,256]{1,0:T(8,128)(2,1)S(1)} %get-tuple-element.30), channel_id=1, source_target_pairs={{0,8},{8,0},{16,24},{24,16},{1,9},{9,1},{17,25},{25,17},{2,10},{10... | collective-permute-start | bytes 786440 | tf_op jit(solution)/shard_map/ppermute | solution.py:307
  65.7 38.9 %collective-permute-start.2 = (bf16[512,256]{1,0:T(8,128)(2,1)S(1)}, bf16[512,256]{1,0:T(8,128)(2,1)S(1)}, u32[]{:S(2)}, u32[]{:S(2)}) collective-permute-start(bf16[512,256]{1,0:T(8,128)(2,1)S(1)} %get-tuple-element.31), channel_id=1, source_target_pairs={{0,16},{8,24},{16,0},{24,8},{1,17},{9,25},{17,1},{25,9},{2,18},{10... | collective-permute-start | bytes 786440 | tf_op jit(solution)/shard_map/ppermute | solution.py:307
  70.7 48.9 %collective-permute-start.3 = (bf16[512,256]{1,0:T(8,128)(2,1)S(1)}, bf16[512,256]{1,0:T(8,128)(2,1)S(1)}, u32[]{:S(2)}, u32[]{:S(2)}) collective-permute-start(bf16[512,256]{1,0:T(8,128)(2,1)S(1)} %get-tuple-element.32), channel_id=1, source_target_pairs={{0,24},{8,16},{16,8},{24,0},{1,25},{9,17},{17,9},{25,1},{2,26},{10... | collective-permute-start | bytes 786440 | tf_op jit(solution)/shard_map/ppermute | solution.py:307
  104.6 29.1 %copy-start = (bf16[512,256]{1,0:T(8,128)(2,1)}, bf16[512,256]{1,0:T(8,128)(2,1)S(1)}, u32[]{:S(2)}) copy-start(bf16[512,256]{1,0:T(8,128)(2,1)S(1)} %collective-permute-done.2.w2) | copy-start | bytes 786436
  121.2 0.7 copy-start.2
  121.9 11.8 %collective-permute-start.4 = (bf16[640,256]{1,0:T(8,128)(2,1)}, bf16[640,256]{1,0:T(8,128)(2,1)}, u32[]{:S(2)}, u32[]{:S(2)}) collective-permute-start(bf16[640,256]{1,0:T(8,128)(2,1)} %shard_map.93.mine), channel_id=1, source_target_pairs={{0,4},{4,0},{1,5},{5,1},{2,6},{6,2},{3,7},{7,3},{8,12},{12,8},{9,1... | collective-permute-start | bytes 983048 | tf_op jit(solution)/shard_map/ppermute | solution.py:307
  133.7 0.7 copy-start.14
  138.4 0.9 copy-start.1
  139.4 0.9 copy-start.3
  140.3 7.3 %copy-start.4 = (bf16[512,256]{1,0:T(8,128)(2,1)S(1)}, bf16[512,256]{1,0:T(8,128)(2,1)}, u32[]{:S(2)}) copy-start(bf16[512,256]{1,0:T(8,128)(2,1)} %copy-done.2) | copy-start | bytes 786436
  141.6 6.1 %collective-permute-start.8 = (bf16[512,2048]{1,0:T(8,128)(2,1)S(1)}, bf16[512,2048]{1,0:T(8,128)(2,1)S(1)}, u32[]{:S(2)}, u32[]{:S(2)}) collective-permute-start(bf16[512,2048]{1,0:T(8,128)(2,1)S(1)} %shard_map.98), channel_id=1, source_target_pairs={{0,32},{32,0},{1,33},{33,1},{2,34},{34,2},{3,35},{35,3},{4,36},{36... | collective-permute-start | bytes 6291464 | tf_op jit(solution)/shard_map/ppermute | solution.py:307
  180.6 9.1 %copy-start.9 = (bf16[32,256]{1,0:T(8,128)(2,1)S(1)}, bf16[32,256]{1,0:T(8,128)(2,1)}, u32[]{:S(2)}) copy-start(bf16[32,256]{1,0:T(8,128)(2,1)} %copy-done.8) | copy-start | bytes 49156
  180.6 9.1 %copy-start.11 = (bf16[32,256]{1,0:T(8,128)(2,1)S(1)}, bf16[32,256]{1,0:T(8,128)(2,1)}, u32[]{:S(2)}) copy-start(bf16[32,256]{1,0:T(8,128)(2,1)} %copy-done.10) | copy-start | bytes 49156
  180.6 9.1 %copy-start.13 = (bf16[32,256]{1,0:T(8,128)(2,1)S(1)}, bf16[32,256]{1,0:T(8,128)(2,1)}, u32[]{:S(2)}) copy-start(bf16[32,256]{1,0:T(8,128)(2,1)} %copy-done.12) | copy-start | bytes 49156
  181.5 68.4 %all-to-all-start.3 = ((bf16[8,16,512]{2,1,0:T(8,128)(2,1)}), bf16[8,16,512]{2,1,0:T(8,128)(2,1)S(1)}, u32[]{:S(2)}, u32[]{:S(2)}) async-start(bf16[8,16,512]{2,1,0:T(8,128)(2,1)} %shard_map.100), calls=%async_computation.3 | async-start | bytes 262144 | tf_op jit(solution)/shard_map/all_to_all | solution.py:310
  191.0 33.0 %collective-permute-start.5 = (bf16[544,256]{1,0:T(8,128)(2,1)S(1)}, bf16[544,256]{1,0:T(8,128)(2,1)S(1)}, u32[]{:S(2)}, u32[]{:S(2)}) collective-permute-start(bf16[544,256]{1,0:T(8,128)(2,1)S(1)} %get-tuple-element.43), channel_id=1, source_target_pairs={{0,8},{8,0},{16,24},{24,16},{1,9},{9,1},{17,25},{25,17},{2,10},{10... | collective-permute-start | bytes 835592 | tf_op jit(solution)/shard_map/ppermute | solution.py:307
  193.0 43.0 %collective-permute-start.6 = (bf16[544,256]{1,0:T(8,128)(2,1)S(1)}, bf16[544,256]{1,0:T(8,128)(2,1)S(1)}, u32[]{:S(2)}, u32[]{:S(2)}) collective-permute-start(bf16[544,256]{1,0:T(8,128)(2,1)S(1)} %get-tuple-element.44), channel_id=1, source_target_pairs={{0,16},{8,24},{16,0},{24,8},{1,17},{9,25},{17,1},{25,9},{2,18},{10... | collective-permute-start | bytes 835592 | tf_op jit(solution)/shard_map/ppermute | solution.py:307
  200.8 47.6 %collective-permute-start.7 = (bf16[544,256]{1,0:T(8,128)(2,1)S(1)}, bf16[544,256]{1,0:T(8,128)(2,1)S(1)}, u32[]{:S(2)}, u32[]{:S(2)}) collective-permute-start(bf16[544,256]{1,0:T(8,128)(2,1)S(1)} %get-tuple-element.45), channel_id=1, source_target_pairs={{0,24},{8,16},{16,8},{24,0},{1,25},{9,17},{17,9},{25,1},{2,26},{10... | collective-permute-start | bytes 835592 | tf_op jit(solution)/shard_map/ppermute | solution.py:307
  (3 other events, 1.8 us)

commit v3 on v2

--- a/solution.py
+++ b/solution.py
@@ -21,7 +21,7 @@
 LANES = 128
 CUT = 256
 BLOCK = 512
-PACK = 176
+PACK = 96
 EXTRA = 32
 
 VMEM = functools.partial(pl.BlockSpec, memory_space=pltpu.VMEM)
@@ -34,9 +34,10 @@
 
 def kernel(body, outs, ins, flops, moved, name):
     ins = [pltpu.with_memory_space_constraint(x, pltpu.VMEM) for x in ins]
+    place = pltpu.VMEM if name in KEEP else pltpu.HBM if name in LEAVE else None
     return pl.pallas_call(
         body,
-        out_shape=jax.tree.map(lambda o: pltpu.VMEM(o.shape, o.dtype), outs) if name in KEEP else outs,
+        out_shape=jax.tree.map(lambda o: place(o.shape, o.dtype), outs) if place else outs,
         in_specs=[VMEM()] * len(ins),
         out_specs=jax.tree.map(lambda _: VMEM(), outs),
         compiler_params=pltpu.CompilerParams(vmem_limit_bytes=20 << 20),
@@ -44,7 +45,8 @@
     )(*ins)
 
 
-KEEP = ("weights", "compact", "logits", "grads", "send", "keep", "plane", "weight_grad", "tables")
+KEEP = ("compact", "logits", "grads", "halves", "plane", "tables")
+LEAVE = ("input",)
 
 
 def home():
@@ -75,11 +77,11 @@
         copy.wait()
 
 
-def packet_body(lengths, hidden_ref, cot_hbm, out, even_ref, odd_ref, cot_ref, sems):
-    spot = (8 * lax.axis_index("y") + lax.axis_index("x")) * LANES
+def packet_body(lengths, hidden_ref, cot_hbm, out, near_ref, far_ref, cot_ref, sems):
+    spot = (4 * lax.axis_index("y") + lax.axis_index("x")) * LANES
     copies = []
-    for i, ref in enumerate((even_ref, odd_ref)):
-        start = pl.multiple_of(spot + i * BLOCK, LANES)
+    for i, ref in enumerate((near_ref, far_ref)):
+        start = pl.multiple_of(spot + i * 2048, LANES)
         copies.append(pltpu.make_async_copy(hidden_ref.at[:, pl.ds(start, LANES)], ref, sems.at[i]))
     copies.append(pltpu.make_async_copy(cot_hbm, cot_ref, sems.at[2]))
     for copy in copies:
@@ -91,46 +93,54 @@
     for s in range(8):
         lens = jnp.where(row == s, lengths[s].astype(F32), lens)
     lens = lens.astype(BF16)
+    first = iota((64, LANES), 1) < 64
+    low_core = lax.axis_index("c") == 0
+    folded = []
+    for ref in (near_ref, far_ref):
+        top, bottom = ref[0:64, :].astype(F32), ref[64:128, :].astype(F32)
+        zero = jnp.where(first, top, pltpu.roll(bottom, 64, 1))
+        one = jnp.where(first, pltpu.roll(top, 64, 1), bottom)
+        folded.append(jnp.where(low_core, zero, one).astype(BF16))
     for a in range(4):
-        high, low = split(cot_ref[:, a * CUT : (a + 1) * CUT])
-        pieces = []
-        for part in (high.astype(F32), low.astype(F32)):
-            pieces.append(jnp.concatenate([part[:, :LANES], part[:, LANES:]], axis=0).astype(BF16))
-        for q, source in enumerate((even_ref, odd_ref)):
-            k = 2 * a + q
-            out[k, 0:128, :] = source[...]
-            out[k, 128:144, :] = lens
-            out[k, 144:160, :] = pieces[0]
-            out[k, 160:176, :] = pieces[1]
+        part = cot_ref[:, a * CUT : (a + 1) * CUT]
+        part = jnp.concatenate([part[:, :LANES], part[:, LANES:]], axis=0).astype(BF16)
+        for q in range(2):
+            k = 4 * q + a
+            out[k, 0:64, :] = folded[q]
+            out[k, 64:80, :] = lens
+            out[k, 80:96, :] = part
 
 
 def compact_body(got, out, cot_out, len_out):
-    at = home()
-    column = jnp.concatenate([got[k, 128:144, :].astype(F32)[0:8] for k in range(8)], axis=0)
+    column = jnp.concatenate([got[k, 64:80, :].astype(F32)[0:8] for k in range(8)], axis=0)
     len_out[...] = column
-    wide = jnp.broadcast_to(column[:, 0:1], (SEQS, TOKENS))
-    seq = iota((SEQS, TOKENS), 0)
-    token = iota((SEQS, TOKENS), 1)
-    start = jnp.sum(jnp.where(seq < token // LEN, wide, 0.0), axis=0, keepdims=True)
-    length = jnp.sum(jnp.where(seq == token // LEN, wide, 0.0), axis=0, keepdims=True)
-    place = iota((1, TOKENS), 1) % LEN
-    spot = jnp.where(place.astype(F32) < length, start.astype(I32) + place, -1)
-    rows = iota((HALF, TOKENS), 0) + at[2] * HALF
-    pick = jnp.where(jnp.broadcast_to(spot, (HALF, TOKENS)) == rows, 1.0, 0.0).astype(BF16)
-    tokens = jnp.concatenate([got[k, 0:128, :] for k in range(8)], axis=0)
-    chosen = dot(pick, tokens).astype(BF16)
+    wide = jnp.broadcast_to(column[:, 0:1], (SEQS, TOKENS // 2))
+    seq = iota((SEQS, TOKENS // 2), 0)
+    index = iota((SEQS, TOKENS // 2), 1)
+    tokens = jnp.concatenate([got[k, 0:64, :] for k in range(8)], axis=0)
+    rows = iota((LIVE, TOKENS // 2), 0)
+    chosen = []
+    for half in range(2):
+        owner = (index // 64) * 8 + half * 4 + (index % 64) // LEN
+        start = jnp.sum(jnp.where(seq < owner, wide, 0.0), axis=0, keepdims=True)
+        length = jnp.sum(jnp.where(seq == owner, wide, 0.0), axis=0, keepdims=True)
+        place = iota((1, TOKENS // 2), 1) % LEN
+        spot = jnp.where(place.astype(F32) < length, start.astype(I32) + place, -1)
+        pick = jnp.where(jnp.broadcast_to(spot, rows.shape) == rows, 1.0, 0.0).astype(BF16)
+        chosen.append(dot(pick, tokens))
+    first = iota((HALF, LANES), 1) < 64
+    early = chosen[0][:HALF] + pltpu.roll(chosen[1][:HALF], 64, 1)
+    late = pltpu.roll(chosen[0][HALF:], 64, 1) + chosen[1][HALF:]
+    folded = jnp.where(first, early, late).astype(BF16)
     for j in range(16):
-        out[j] = chosen
+        out[j] = folded
     for k in range(8):
-        high = got[k, 144:160, :].astype(F32)
-        low = got[k, 160:176, :].astype(F32)
-        both = high + low
-        cot_out[k * 8 : (k + 1) * 8, 0:LANES] = both[0:8]
-        cot_out[k * 8 : (k + 1) * 8, LANES:CUT] = both[8:16]
+        cot = got[k, 80:96, :].astype(F32)
+        cot_out[k * 8 : (k + 1) * 8, 0:LANES] = cot[0:8]
+        cot_out[k * 8 : (k + 1) * 8, LANES:CUT] = cot[8:16]
 
 
 def tables_body(len_ref, seg_ref, segt_ref, spread_ref):
-    at = home()
     lens = len_ref[...]
     sub = iota((SEQS, LANES), 0)
     lane = iota((SEQS, LANES), 1)
@@ -150,8 +160,7 @@
     segt_ref[...] = jnp.where(inside, 1.0, 0.0).astype(BF16)
     row = iota((TOKENS, LANES), 0)
     lane = iota((TOKENS, LANES), 1)
-    core = (row >> 9) ^ at[2]
-    which = (((((row >> 4) & 1) * 4 + ((row >> 7) & 3)) * 2 + core) * 4) + ((row >> 5) & 3)
+    which = ((((row >> 5) & 1) * 4 + (row >> 8)) * 2 + ((row >> 4) & 1)) * 4 + ((row >> 6) & 3)
     per_row = jnp.broadcast_to(len_row, (TOKENS, LANES))
     start = jnp.sum(jnp.where(lane < which, per_row, 0.0), axis=1, keepdims=True)
     length = jnp.sum(jnp.where(lane == which, per_row, 0.0), axis=1, keepdims=True)
@@ -161,18 +170,29 @@
     spread_ref[...] = jnp.where(jnp.broadcast_to(spot, (TOKENS, LIVE)) == target, 1.0, 0.0).astype(BF16)
 
 
-def wide_rows(ref, block):
-    return jnp.concatenate([ref[block * 4 + i] for i in range(4)], axis=1)
-
-
-def logits_body(own, other, w0, w1, w2, w3, out):
-    at = home()
-    for hop, ref in enumerate((own, other)):
-        total = jnp.zeros((HALF, CUT), F32)
-        for m, w in enumerate((w0, w1, w2, w3)):
-            total = total + dot(wide_rows(ref, at[0] ^ m), w[...])
-        half = at[2] ^ hop
-        out[pl.ds(pl.multiple_of(half * HALF, HALF), HALF), :] = total.astype(BF16)
+def logits_body(own, other, w0, w1, w2, w3, out, rows_out):
+    at = home()
+
+    def unfold(low, high):
+        first = iota((HALF, LANES), 1) < 64
+        for j in range(16):
+            left, right = low[j], high[j]
+            columns = pl.ds((j % 4) * LANES, LANES)
+            rows_out[j // 4, 0:HALF, columns] = jnp.where(first, left, pltpu.roll(right, 64, 1))
+            rows_out[j // 4, HALF:LIVE, columns] = jnp.where(first, pltpu.roll(left, 64, 1), right)
+
+    @pl.when(at[2] == 0)
+    def _():
+        unfold(own, other)
+
+    @pl.when(at[2] == 1)
+    def _():
+        unfold(other, own)
+
+    total = jnp.zeros((LIVE, CUT), F32)
+    for m, w in enumerate((w0, w1, w2, w3)):
+        total = total + dot(rows_out[at[0] ^ m], w[...])
+    out[...] = total.astype(BF16)
 
 
 def grads_body(mine, theirs, bias, cot, seg, segt, grad_out, x0, x1, x2, x3):
@@ -203,7 +223,7 @@
         tail = jnp.where(row == i, jnp.broadcast_to(v.astype(F32), (16, CUT)), tail)
     tail = tail.astype(BF16)
     for m, out in enumerate((x0, x1, x2, x3)):
-        k = (at[0] ^ m) * 2 + at[1]
+        k = at[1] * 4 + (at[0] ^ m)
         mine8 = jnp.zeros((8, CUT), F32)
         for i in range(8):
             mine8 = jnp.where(k == i, pooled[i * 8 : (i + 1) * 8], mine8)
@@ -212,33 +232,28 @@
         out[16:32, :] = tail
 
 
-def weight_grad_body(own, other, grad, x0, x1, x2, x3, o0, o1, o2, o3):
+def weight_grad_body(rows, grad, x0, x1, x2, x3, o0, o1, o2, o3):
     at = home()
     for m, (extra, out) in enumerate(zip((x0, x1, x2, x3), (o0, o1, o2, o3))):
-        total = jnp.zeros((BLOCK, CUT), F32)
-        for hop, ref in enumerate((own, other)):
-            half = at[2] ^ hop
-            part = grad[pl.ds(pl.multiple_of(half * HALF, HALF), HALF), :]
-            total = total + dot(wide_rows(ref, at[0] ^ m), part, ((0,), (0,)))
-        out[0:BLOCK, :] = total.astype(BF16)
+        out[0:BLOCK, :] = dot(rows[at[0] ^ m], grad[...], ((0,), (0,))).astype(BF16)
         out[BLOCK : BLOCK + EXTRA, :] = extra[...]
 
 
-def send_body(spread, grad, w0, w1, w2, w3, out):
-    at = home()
-    rows = dot(spread[TOKENS // 2 :, :], grad[...]).astype(BF16)
+def halves_body(w0, w1, w2, w3, out):
+    start = pl.multiple_of((1 - lax.axis_index("c")) * CUT, CUT)
     for m, w in enumerate((w0, w1, w2, w3)):
-        start = pl.multiple_of((at[0] ^ m) * BLOCK, BLOCK)
-        out[:, pl.ds(start, BLOCK)] = dot(rows, w[...], ((1,), (1,))).astype(BF16)
-
-
-def keep_body(spread, grad, w0, w1, w2, w3, got, out):
-    at = home()
-    rows = dot(spread[: TOKENS // 2, :], grad[...]).astype(BF16)
+        out[m] = w[pl.ds(start, CUT), :]
+
+
+def input_body(spread, grad, partner, w0, w1, w2, w3, half, out):
+    at = home()
+    start = pl.multiple_of(at[2] * CUT, CUT)
+    mine = dot(spread[...], grad[...]).astype(BF16)
+    theirs = dot(spread[...], partner[...]).astype(BF16)
     for m, w in enumerate((w0, w1, w2, w3)):
-        start = pl.multiple_of((at[0] ^ m) * BLOCK, BLOCK)
-        part = dot(rows, w[...], ((1,), (1,)))
-        out[:, pl.ds(start, BLOCK)] = (part + got[:, pl.ds(start, BLOCK)].astype(F32)).astype(BF16)
+        total = dot(mine, w[pl.ds(start, CUT), :], ((1,), (1,)))
+        total = total + dot(theirs, half[m], ((1,), (1,)))
+        out[:, pl.ds(pl.multiple_of((at[0] ^ m) * CUT, CUT), CUT)] = total.astype(BF16)
 
 
 def plane_body(got, out):
@@ -247,15 +262,19 @@
         total = total + got[i].astype(F32)
     total = total.astype(BF16)
     for zh in range(2):
-        for a in range(4):
-            out[zh * 4 + a] = total[zh * 16 : (zh + 1) * 16, a * BLOCK : (a + 1) * BLOCK]
+        for core in range(2):
+            start = zh * 32 + core * 16
+            for a in range(4):
+                out[zh * 8 + core * 4 + a] = total[start : start + 16, a * CUT : (a + 1) * CUT]
 
 
 def last_body(got, out):
-    total = got[0].astype(F32)
-    for i in range(1, 8):
-        total = total + got[i].astype(F32)
-    out[...] = total
+    for core in range(2):
+        total = jnp.zeros((16, CUT), F32)
+        for zh in range(2):
+            for a in range(4):
+                total = total + got[zh * 8 + core * 4 + a].astype(F32)
+        out[:, core * CUT : (core + 1) * CUT] = total
 
 
 def unpack_body(p0, p1, p2, p3, weight_out, pooled_out, mean_out, bias_out):
@@ -267,6 +286,10 @@
         pooled_out[:, columns] = extra[0:8] + extra[8:16]
         mean_out[:, columns] = extra[16:17] + extra[17:18]
         bias_out[:, columns] = extra[18:19] + extra[19:20]
+
+
+def here(value):
+    return pltpu.with_memory_space_constraint(value, pltpu.HBM)
 
 
 def pack(lengths, hidden, rep_cotangent):
@@ -283,7 +306,7 @@
         ],
         compiler_params=pltpu.CompilerParams(vmem_limit_bytes=8 << 20),
         name="packet",
-    )(lengths, hidden, rep_cotangent)
+    )(here(lengths), here(hidden), here(rep_cotangent))
 
 
 def cut(head_weight):
@@ -295,7 +318,7 @@
         scratch_shapes=[pltpu.SemaphoreType.DMA((4,))],
         compiler_params=pltpu.CompilerParams(vmem_limit_bytes=8 << 20),
         name="weights",
-    )(head_weight)
+    )(here(head_weight))
 
 
 def shape(dims, kind=BF16):
@@ -313,7 +336,7 @@
     w = [w[0]] + [swap(w[m], "zq", 4, m) for m in (1, 2, 3)]
 
     packets = pack(lengths, hidden, rep_cotangent)
-    got = trade(packets, ("zq", "zp"))
+    got = trade(packets, ("zp", "zq"))
     rows, cot, lens = call(
         compact_body,
         [shape((16, HALF, LANES)), shape((SEQS, CUT), F32), shape((SEQS, LANES), F32)],
@@ -330,35 +353,44 @@
         moved=2_000_000,
         name="tables",
     )
-    mine = call(
-        logits_body, shape((LIVE, CUT)), [own, other, *w], 2 * LIVE * 2048 * CUT, 4 << 20, name="logits"
+    mine, all_rows = call(
+        logits_body,
+        [shape((LIVE, CUT)), shape((4, LIVE, BLOCK))],
+        [own, other, *w],
+        2 * LIVE * 2048 * CUT,
+        4 << 20,
+        name="logits",
     )
     theirs = swap(mine, "zp", 2, 1)
+    halves = call(halves_body, shape((4, CUT, CUT)), w, 0, 1 << 20, name="halves")
+    halves = swap(halves, "c", 2, 1)
     grad, *extra = call(
         grads_body,
         [shape((LIVE, CUT))] + [shape((EXTRA, CUT))] * 4,
         [mine, theirs, head_bias.reshape(4, CUT), cot, seg, segt],
         name="grads",
     )
-    send = call(
-        send_body, shape((512, 2048)), [spread, grad, *w], 2 * 512 * 2048 * CUT, 4 << 20, name="send"
-    )
-    came = swap(send, "c", 2, 1)
+    partner = swap(grad, "c", 2, 1)
     pieces = call(
         weight_grad_body,
         [shape((BLOCK + EXTRA, CUT))] * 4,
-        [own, other, grad, *extra],
+        [all_rows, grad, *extra],
         2 * LIVE * 2048 * CUT,
         4 << 20,
         name="weight_grad",
     )
     pieces = [pieces[0]] + [swap(pieces[m], "zq", 4, m) for m in (1, 2, 3)]
-    kept = call(
-        keep_body, shape((512, 2048)), [spread, grad, *w, came], 2 * 512 * 2048 * CUT, 6 << 20, name="keep"
-    )
-    plane = trade(kept.reshape(16, 32, 2048), ("y", "x"))
-    column = call(plane_body, shape((8, 16, BLOCK)), [plane], name="plane")
-    column = trade(column, ("zh", "zq"))
+    product = call(
+        input_body,
+        shape((TOKENS, 1024)),
+        [spread, grad, partner, *w, halves],
+        2 * TOKENS * 1024 * BLOCK,
+        4 << 20,
+        name="input",
+    )
+    plane = trade(product.reshape(16, 64, 1024), ("y", "x"))
+    column = call(plane_body, shape((16, 16, CUT)), [plane], name="plane")
+    column = trade(column, ("zh", "c", "zq"))
     input_grad = call(last_body, shape((16, BLOCK), F32), [column], name="last")
     weight_grad, pooled, mean, bias_grad = call(
         unpack_body,
@@ -370,8 +402,8 @@
 
 
 def solution(mesh):
-    fine = Mesh(mesh.devices.reshape(2, 4, 2, 4, 2, 4), ("zh", "y", "c", "zq", "zp", "x"))
-    dp = ("zq", "zp")
+    fine = Mesh(mesh.devices.reshape(2, 4, 2, 2, 4, 4), ("zh", "y", "c", "zp", "zq", "x"))
+    dp = ("zp", "zq")
     columns = ("zh", "y", "c", "x")
 
     return jax.shard_map(

time: 251 us -> 209 us (0.83)
  waiting for transfers between devices: 102 us -> 59.6 us
  starting transfers between devices: 38.3 us -> 46.4 us
  local copies, waits for them, and re-layouts: 8.35 us -> 0.97 us
  blocking collectives: 88.7 us -> 82.4 us
  Pallas kernels: 12.8 us -> 18.4 us
    ppermute x9 -> x10, waiting for transfers between devices: 102 us -> 59.6 us  [swap(): return lax.ppermute(value, axis, [(i, i ^ m) for i in range(size)])]
    all_to_all x1, starting transfers between devices: 8.15 us -> 17.3 us  [trade(): return lax.all_to_all(value, axes, 0, 0, tiled=True)]
    unnamed x34 -> x10, local copies, waits for them, and re-layouts: 7.75 us -> 0.97 us
    all_to_all x3, blocking collectives: 88.7 us -> 82.4 us  [trade(): return lax.all_to_all(value, axes, 0, 0, tiled=True)]
    pallas_call x10, Pallas kernels: 11.9 us -> 15.6 us  [kernel(): pl.pallas_call(body, out_shape=jax.tree.map(lambda o: place(o.shape, o.dt...]
    ppermute x9 -> x10, starting transfers between devices: 30.2 us -> 29.2 us  [swap(): return lax.ppermute(value, axis, [(i, i ^ m) for i in range(size)])]
  transfers between devices with their start and end apart: 10 -> 11, of which waited for: 8 -> 8; matrix products, arithmetic and copies ran while one was open for 0% -> 0% of each run, Pallas kernels for 2% -> 4%
where the time goes in v3:
time: 209 us
  blocking collectives  82.4 us (39%)
  waiting for transfers between devices  59.6 us (29%)
  starting transfers between devices  46.4 us (22%)
  Pallas kernels  18.4 us (9%)
    all_to_all x3, blocking collectives, trade(): return lax.all_to_all(value, axes, 0, 0, tiled=True)  82.4 us
    ppermute x10, waiting for transfers between devices, swap(): return lax.ppermute(value, axis, [(i, i ^ m) for i in range(size)])  59.6 us
    ppermute x10, starting transfers between devices, swap(): return lax.ppermute(value, axis, [(i, i ^ m) for i in range(size)])  29.2 us
    all_to_all x1, starting transfers between devices, trade(): return lax.all_to_all(value, axes, 0, 0, tiled=True)  17.3 us
    pallas_call x10, Pallas kernels, kernel(): pl.pallas_call(body, out_shape=jax.tree.map(lambda o: place(o.shape, o.dt...  15.6 us
  transfers between devices with their start and end apart: 11, of which 8 were waited for; matrix products, arithmetic and copies ran while one was open for 0% of the time, Pallas kernels for 4%

profile of v3, /device:TPU:64, one launch (start us, length us, event | category | flops | bytes accessed | tf_op | source)
XLA Modules:
  0.0 208.7 jit_solution(2159496788934345733)
XLA Ops:
  2.2 24.4 %all_to_all.20.got = bf16[8,96,128]{2,1,0:T(8,128)(2,1)S(1)} all-to-all(bf16[8,96,128]{2,1,0:T(8,128)(2,1)S(1)} %packet.1), channel_id=1, replica_groups=mesh['zh'=2,'y'=4,'c'=2,'zp'=2,'zq'=4,'x'=4] {'zp','zq'}, dimensions={0} | all-to-all | bytes 393216 | tf_op jit(solution)/shard_map/all_to_all | solution.py:333
  27.4 25.2 %all_to_all.21.own = bf16[16,320,128]{2,1,0:T(8,128)(2,1)S(1)} all-to-all(bf16[16,320,128]{2,1,0:T(8,128)(2,1)S(1)} %get-tuple-element.30), channel_id=1, replica_groups=mesh['zh'=2,'y'=4,'c'=2,'zp'=2,'zq'=4,'x'=4] {'y','x'}, dimensions={0} | all-to-all | bytes 2621440 | tf_op jit(solution)/shard_map/all_to_all | solution.py:333
  52.6 1.9 collective-permute-start
  55.8 1.9 collective-permute-start.1
  57.7 2.0 collective-permute-start.2
  59.7 5.3 %collective-permute-start.3 = (bf16[512,256]{1,0:T(8,128)(2,1)S(1)}, bf16[512,256]{1,0:T(8,128)(2,1)S(1)}, u32[]{:S(2)}, u32[]{:S(2)}) collective-permute-start(bf16[512,256]{1,0:T(8,128)(2,1)S(1)} %get-tuple-element.34), channel_id=1, source_target_pairs={{0,12},{4,8},{8,4},{12,0},{1,13},{5,9},{9,5},{13,1},{2,14},{6,10},... | collective-permute-start | bytes 786440 | tf_op jit(solution)/shard_map/ppermute | solution.py:330
  65.0 1.8 collective-permute-done.1.w1
  66.9 10.8 %collective-permute-done.2.w2 = bf16[512,256]{1,0:T(8,128)(2,1)S(1)} collective-permute-done((bf16[512,256]{1,0:T(8,128)(2,1)S(1)}, bf16[512,256]{1,0:T(8,128)(2,1)S(1)}, u32[]{:S(2)}, u32[]{:S(2)}) %collective-permute-start.2) | collective-permute-done | bytes 262176 | tf_op jit(solution)/shard_map/ppermute | solution.py:330
  77.7 8.7 %collective-permute-done.3.w3 = bf16[512,256]{1,0:T(8,128)(2,1)S(1)} collective-permute-done((bf16[512,256]{1,0:T(8,128)(2,1)S(1)}, bf16[512,256]{1,0:T(8,128)(2,1)S(1)}, u32[]{:S(2)}, u32[]{:S(2)}) %collective-permute-start.3) | collective-permute-done | bytes 262176 | tf_op jit(solution)/shard_map/ppermute | solution.py:330
  86.4 2.3 %shard_map.93 = (bf16[640,256]{1,0:T(8,128)(2,1)}, bf16[4,640,512]{2,1,0:T(8,128)(2,1)S(1)}) custom-call(bf16[16,320,128]{2,1,0:T(8,128)(2,1)S(1)} %all_to_all.21.own, bf16[16,320,128]{2,1,0:T(8,128)(2,1)S(1)} %collective-permute-done.other, bf16[512,256]{1,0:T(8,128)(2,1)S(1)} %get-tuple-element.31.w0, bf16[512,256]{1,0:T(8,128)(2,1)S(1)} %collective-permute-done.1.w1, ...), custom_call_target="tpu_custom_call" | custom-call | flops 671088640 | bytes 4194304 | tf_op jit(solution)/shard_map/pallas_call | solution.py:38
  88.7 5.0 %collective-permute-start.4 = (bf16[640,256]{1,0:T(8,128)(2,1)}, bf16[640,256]{1,0:T(8,128)(2,1)}, u32[]{:S(2)}, u32[]{:S(2)}) collective-permute-start(bf16[640,256]{1,0:T(8,128)(2,1)} %get-tuple-element.36.mine), channel_id=1, source_target_pairs={{0,16},{16,0},{1,17},{17,1},{2,18},{18,2},{3,19},{19,3},{4,20},{20... | collective-permute-start | bytes 983048 | tf_op jit(solution)/shard_map/ppermute | solution.py:330
  94.5 1.9 collective-permute-start.9
  97.2 12.9 %collective-permute-done.4.theirs = bf16[640,256]{1,0:T(8,128)(2,1)} collective-permute-done((bf16[640,256]{1,0:T(8,128)(2,1)}, bf16[640,256]{1,0:T(8,128)(2,1)}, u32[]{:S(2)}, u32[]{:S(2)}) %collective-permute-start.4) | collective-permute-done | bytes 327712 | tf_op jit(solution)/shard_map/ppermute | solution.py:330
  110.1 2.2 %shard_map.95 = (bf16[640,256]{1,0:T(8,128)(2,1)S(1)}, bf16[32,256]{1,0:T(8,128)(2,1)S(1)}, bf16[32,256]{1,0:T(8,128)(2,1)S(1)}, bf16[32,256]{1,0:T(8,128)(2,1)S(1)}, bf16[32,256]{1,0:T(8,128)(2,1)S(1)}) custom-call(bf16[640,256]{1,0:T(8,128)(2,1)} %get-tuple-element.36.mine, bf16[640,256]{1,0:T(8,128)(2,1)} %collective-permute-done.4.theirs, ...), custom_call_target="tpu_custom_call" | custom-call | tf_op jit(solution)/shard_map/pallas_call | solution.py:38
  112.4 1.9 collective-permute-start.8
  116.8 4.6 %shard_map.99 = bf16[1024,1024]{1,0:T(8,128)(2,1)} custom-call(bf16[1024,640]{1,0:T(8,128)(2,1)S(1)} %get-tuple-element.54.spread, bf16[640,256]{1,0:T(8,128)(2,1)S(1)} %get-tuple-element.41.grad, bf16[640,256]{1,0:T(8,128)(2,1)S(1)} %collective-permute-done.8.partner, bf16[512,256]{1,0:T(8,128)(2,1)S(1)} %get-tuple-element.31.w0, ...), custom_call_target="tpu_custom_call" | custom-call | flops 1073741824 | bytes 4194304 | tf_op jit(solution)/shard_map/pallas_call | solution.py:38
  121.4 32.8 %all_to_all.22.got = bf16[16,64,1024]{2,1,0:T(8,128)(2,1)S(1)} all-to-all(bf16[16,64,1024]{2,1,0:T(8,128)(2,1)} %bitcast.3), channel_id=1, replica_groups=mesh['zh'=2,'y'=4,'c'=2,'zp'=2,'zq'=4,'x'=4] {'y','x'}, dimensions={0} | all-to-all | bytes 4194304 | tf_op jit(solution)/shard_map/all_to_all | solution.py:333
  155.1 17.3 %all-to-all-start.3 = ((bf16[16,16,256]{2,1,0:T(8,128)(2,1)}), bf16[16,16,256]{2,1,0:T(8,128)(2,1)S(1)}, u32[]{:S(2)}, u32[]{:S(2)}) async-start(bf16[16,16,256]{2,1,0:T(8,128)(2,1)} %shard_map.100), calls=%async_computation.3 | async-start | bytes 262144 | tf_op jit(solution)/shard_map/all_to_all | solution.py:333
  173.4 3.4 %collective-permute-start.5 = (bf16[544,256]{1,0:T(8,128)(2,1)S(1)}, bf16[544,256]{1,0:T(8,128)(2,1)S(1)}, u32[]{:S(2)}, u32[]{:S(2)}) collective-permute-start(bf16[544,256]{1,0:T(8,128)(2,1)S(1)} %get-tuple-element.47), channel_id=1, source_target_pairs={{0,4},{4,0},{8,12},{12,8},{1,5},{5,1},{9,13},{13,9},{2,6},{6,2},{1... | collective-permute-start | bytes 835592 | tf_op jit(solution)/shard_map/ppermute | solution.py:330
  176.8 2.5 %collective-permute-start.6 = (bf16[544,256]{1,0:T(8,128)(2,1)S(1)}, bf16[544,256]{1,0:T(8,128)(2,1)S(1)}, u32[]{:S(2)}, u32[]{:S(2)}) collective-permute-start(bf16[544,256]{1,0:T(8,128)(2,1)S(1)} %get-tuple-element.48), channel_id=1, source_target_pairs={{0,8},{4,12},{8,0},{12,4},{1,9},{5,13},{9,1},{13,5},{2,10},{6,14},... | collective-permute-start | bytes 835592 | tf_op jit(solution)/shard_map/ppermute | solution.py:330
  179.3 3.4 %collective-permute-start.7 = (bf16[544,256]{1,0:T(8,128)(2,1)S(1)}, bf16[544,256]{1,0:T(8,128)(2,1)S(1)}, u32[]{:S(2)}, u32[]{:S(2)}) collective-permute-start(bf16[544,256]{1,0:T(8,128)(2,1)S(1)} %get-tuple-element.49), channel_id=1, source_target_pairs={{0,12},{4,8},{8,4},{12,0},{1,13},{5,9},{9,5},{13,1},{2,14},{6,10},... | collective-permute-start | bytes 835592 | tf_op jit(solution)/shard_map/ppermute | solution.py:330
  182.7 8.6 %collective-permute-done.5.p1 = bf16[544,256]{1,0:T(8,128)(2,1)S(1)} collective-permute-done((bf16[544,256]{1,0:T(8,128)(2,1)S(1)}, bf16[544,256]{1,0:T(8,128)(2,1)S(1)}, u32[]{:S(2)}, u32[]{:S(2)}) %collective-permute-start.5) | collective-permute-done | bytes 278560 | tf_op jit(solution)/shard_map/ppermute | solution.py:330
  191.3 7.7 %collective-permute-done.6.p2 = bf16[544,256]{1,0:T(8,128)(2,1)S(1)} collective-permute-done((bf16[544,256]{1,0:T(8,128)(2,1)S(1)}, bf16[544,256]{1,0:T(8,128)(2,1)S(1)}, u32[]{:S(2)}, u32[]{:S(2)}) %collective-permute-start.6) | collective-permute-done | bytes 278560 | tf_op jit(solution)/shard_map/ppermute | solution.py:330
  199.0 7.6 %collective-permute-done.7.p3 = bf16[544,256]{1,0:T(8,128)(2,1)S(1)} collective-permute-done((bf16[544,256]{1,0:T(8,128)(2,1)S(1)}, bf16[544,256]{1,0:T(8,128)(2,1)S(1)}, u32[]{:S(2)}, u32[]{:S(2)}) %collective-permute-start.7) | collective-permute-done | bytes 278560 | tf_op jit(solution)/shard_map/ppermute | solution.py:330
  (24 shorter events, 11.9 us)
Async XLA Ops:
  52.6 33.7 %collective-permute-start = (bf16[16,320,128]{2,1,0:T(8,128)(2,1)S(1)}, bf16[16,320,128]{2,1,0:T(8,128)(2,1)S(1)}, u32[]{:S(2)}, u32[]{:S(2)}) collective-permute-start(bf16[16,320,128]{2,1,0:T(8,128)(2,1)S(1)} %all_to_all.21.own), channel_id=1, source_target_pairs={{0,32},{32,0},{1,33},{33,1},{2,34},{34,2},{3,35},{35,3},{4,36},{36... | collective-permute-start | bytes 3932168 | tf_op jit(solution)/shard_map/ppermute | solution.py:330
  55.8 11.1 %collective-permute-start.1 = (bf16[512,256]{1,0:T(8,128)(2,1)S(1)}, bf16[512,256]{1,0:T(8,128)(2,1)S(1)}, u32[]{:S(2)}, u32[]{:S(2)}) collective-permute-start(bf16[512,256]{1,0:T(8,128)(2,1)S(1)} %get-tuple-element.32), channel_id=1, source_target_pairs={{0,4},{4,0},{8,12},{12,8},{1,5},{5,1},{9,13},{13,9},{2,6},{6,2},{1... | collective-permute-start | bytes 786440 | tf_op jit(solution)/shard_map/ppermute | solution.py:330
  57.7 19.9 %collective-permute-start.2 = (bf16[512,256]{1,0:T(8,128)(2,1)S(1)}, bf16[512,256]{1,0:T(8,128)(2,1)S(1)}, u32[]{:S(2)}, u32[]{:S(2)}) collective-permute-start(bf16[512,256]{1,0:T(8,128)(2,1)S(1)} %get-tuple-element.33), channel_id=1, source_target_pairs={{0,8},{4,12},{8,0},{12,4},{1,9},{5,13},{9,1},{13,5},{2,10},{6,14},... | collective-permute-start | bytes 786440 | tf_op jit(solution)/shard_map/ppermute | solution.py:330
  59.7 26.6 %collective-permute-start.3 = (bf16[512,256]{1,0:T(8,128)(2,1)S(1)}, bf16[512,256]{1,0:T(8,128)(2,1)S(1)}, u32[]{:S(2)}, u32[]{:S(2)}) collective-permute-start(bf16[512,256]{1,0:T(8,128)(2,1)S(1)} %get-tuple-element.34), channel_id=1, source_target_pairs={{0,12},{4,8},{8,4},{12,0},{1,13},{5,9},{9,5},{13,1},{2,14},{6,10},... | collective-permute-start | bytes 786440 | tf_op jit(solution)/shard_map/ppermute | solution.py:330
  86.3 8.2 %copy-start = (bf16[512,256]{1,0:T(8,128)(2,1)}, bf16[512,256]{1,0:T(8,128)(2,1)S(1)}, u32[]{:S(2)}) copy-start(bf16[512,256]{1,0:T(8,128)(2,1)S(1)} %collective-permute-done.3.w3) | copy-start | bytes 786436
  86.4 10.1 %copy-start.4 = (f32[1024]{0:T(1024)S(1)}, f32[1024]{0:T(1024)}, u32[]{:S(2)}) copy-start(f32[1024]{0:T(1024)} %param.7) | copy-start | bytes 12292
  88.7 21.5 %collective-permute-start.4 = (bf16[640,256]{1,0:T(8,128)(2,1)}, bf16[640,256]{1,0:T(8,128)(2,1)}, u32[]{:S(2)}, u32[]{:S(2)}) collective-permute-start(bf16[640,256]{1,0:T(8,128)(2,1)} %get-tuple-element.36.mine), channel_id=1, source_target_pairs={{0,16},{16,0},{1,17},{17,1},{2,18},{18,2},{3,19},{19,3},{4,20},{20... | collective-permute-start | bytes 983048 | tf_op jit(solution)/shard_map/ppermute | solution.py:330
  94.5 19.8 %collective-permute-start.9 = (bf16[4,256,256]{2,1,0:T(8,128)(2,1)}, bf16[4,256,256]{2,1,0:T(8,128)(2,1)}, u32[]{:S(2)}, u32[]{:S(2)}) collective-permute-start(bf16[4,256,256]{2,1,0:T(8,128)(2,1)} %shard_map.98), channel_id=1, source_target_pairs={{0,32},{32,0},{1,33},{33,1},{2,34},{34,2},{3,35},{35,3},{4,36},{36... | collective-permute-start | bytes 1572872 | tf_op jit(solution)/shard_map/ppermute | solution.py:330
  112.4 9.1 %copy-start.2 = (bf16[640,256]{1,0:T(8,128)(2,1)}, bf16[640,256]{1,0:T(8,128)(2,1)S(1)}, u32[]{:S(2)}) copy-start(bf16[640,256]{1,0:T(8,128)(2,1)S(1)} %get-tuple-element.41.grad) | copy-start | bytes 983044
  112.4 3.5 %collective-permute-start.8 = (bf16[640,256]{1,0:T(8,128)(2,1)S(1)}, bf16[640,256]{1,0:T(8,128)(2,1)S(1)}, u32[]{:S(2)}, u32[]{:S(2)}) collective-permute-start(bf16[640,256]{1,0:T(8,128)(2,1)S(1)} %get-tuple-element.41.grad), channel_id=1, source_target_pairs={{0,32},{32,0},{1,33},{33,1},{2,34},{34,2},{3,35},{35,3},{4,36},{36... | collective-permute-start | bytes 983048 | tf_op jit(solution)/shard_map/ppermute | solution.py:330
  115.9 1.0 copy-start.1
  154.2 18.2 %copy-start.3 = (bf16[640,256]{1,0:T(8,128)(2,1)S(1)}, bf16[640,256]{1,0:T(8,128)(2,1)}, u32[]{:S(2)}) copy-start(bf16[640,256]{1,0:T(8,128)(2,1)} %copy-done.2) | copy-start | bytes 983044
  155.1 52.9 %all-to-all-start.3 = ((bf16[16,16,256]{2,1,0:T(8,128)(2,1)}), bf16[16,16,256]{2,1,0:T(8,128)(2,1)S(1)}, u32[]{:S(2)}, u32[]{:S(2)}) async-start(bf16[16,16,256]{2,1,0:T(8,128)(2,1)} %shard_map.100), calls=%async_computation.3 | async-start | bytes 262144 | tf_op jit(solution)/shard_map/all_to_all | solution.py:333
  173.4 17.9 %collective-permute-start.5 = (bf16[544,256]{1,0:T(8,128)(2,1)S(1)}, bf16[544,256]{1,0:T(8,128)(2,1)S(1)}, u32[]{:S(2)}, u32[]{:S(2)}) collective-permute-start(bf16[544,256]{1,0:T(8,128)(2,1)S(1)} %get-tuple-element.47), channel_id=1, source_target_pairs={{0,4},{4,0},{8,12},{12,8},{1,5},{5,1},{9,13},{13,9},{2,6},{6,2},{1... | collective-permute-start | bytes 835592 | tf_op jit(solution)/shard_map/ppermute | solution.py:330
  176.8 22.1 %collective-permute-start.6 = (bf16[544,256]{1,0:T(8,128)(2,1)S(1)}, bf16[544,256]{1,0:T(8,128)(2,1)S(1)}, u32[]{:S(2)}, u32[]{:S(2)}) collective-permute-start(bf16[544,256]{1,0:T(8,128)(2,1)S(1)} %get-tuple-element.48), channel_id=1, source_target_pairs={{0,8},{4,12},{8,0},{12,4},{1,9},{5,13},{9,1},{13,5},{2,10},{6,14},... | collective-permute-start | bytes 835592 | tf_op jit(solution)/shard_map/ppermute | solution.py:330
  179.3 27.2 %collective-permute-start.7 = (bf16[544,256]{1,0:T(8,128)(2,1)S(1)}, bf16[544,256]{1,0:T(8,128)(2,1)S(1)}, u32[]{:S(2)}, u32[]{:S(2)}) collective-permute-start(bf16[544,256]{1,0:T(8,128)(2,1)S(1)} %get-tuple-element.49), channel_id=1, source_target_pairs={{0,12},{4,8},{8,4},{12,0},{1,13},{5,9},{9,5},{13,1},{2,14},{6,10},... | collective-permute-start | bytes 835592 | tf_op jit(solution)/shard_map/ppermute | solution.py:330

commit v4 on v3

--- a/solution.py
+++ b/solution.py
@@ -18,6 +18,7 @@
 TOKENS = SEQS * LEN
 LIVE = SEQS * LEN * 5 // 8
 HALF = LIVE // 2
+QUART = LIVE // 4
 LANES = 128
 CUT = 256
 BLOCK = 512
@@ -33,7 +34,8 @@
 
 
 def kernel(body, outs, ins, flops, moved, name):
-    ins = [pltpu.with_memory_space_constraint(x, pltpu.VMEM) for x in ins]
+    if name not in FREE:
+        ins = [pltpu.with_memory_space_constraint(x, pltpu.VMEM) for x in ins]
     place = pltpu.VMEM if name in KEEP else pltpu.HBM if name in LEAVE else None
     return pl.pallas_call(
         body,
@@ -45,8 +47,9 @@
     )(*ins)
 
 
-KEEP = ("compact", "logits", "grads", "halves", "plane", "tables")
+KEEP = ("compact", "grads", "halves", "plane", "tables")
 LEAVE = ("input",)
+FREE = ("weight_grad", "unpack")
 
 
 def home():
@@ -111,7 +114,7 @@
             out[k, 80:96, :] = part
 
 
-def compact_body(got, out, cot_out, len_out):
+def compact_body(got, out_a, out_b, cot_out, len_out):
     column = jnp.concatenate([got[k, 64:80, :].astype(F32)[0:8] for k in range(8)], axis=0)
     len_out[...] = column
     wide = jnp.broadcast_to(column[:, 0:1], (SEQS, TOKENS // 2))
@@ -128,12 +131,14 @@
         spot = jnp.where(place.astype(F32) < length, start.astype(I32) + place, -1)
         pick = jnp.where(jnp.broadcast_to(spot, rows.shape) == rows, 1.0, 0.0).astype(BF16)
         chosen.append(dot(pick, tokens))
-    first = iota((HALF, LANES), 1) < 64
-    early = chosen[0][:HALF] + pltpu.roll(chosen[1][:HALF], 64, 1)
-    late = pltpu.roll(chosen[0][HALF:], 64, 1) + chosen[1][HALF:]
-    folded = jnp.where(first, early, late).astype(BF16)
-    for j in range(16):
-        out[j] = folded
+    first = iota((QUART, LANES), 1) < 64
+    for part, out in enumerate((out_a, out_b)):
+        start, middle, end = part * HALF, part * HALF + QUART, part * HALF + HALF
+        early = chosen[0][start:middle] + pltpu.roll(chosen[1][start:middle], 64, 1)
+        late = pltpu.roll(chosen[0][middle:end], 64, 1) + chosen[1][middle:end]
+        folded = jnp.where(first, early, late).astype(BF16)
+        for j in range(16):
+            out[j] = folded
     for k in range(8):
         cot = got[k, 80:96, :].astype(F32)
         cot_out[k * 8 : (k + 1) * 8, 0:LANES] = cot[0:8]
@@ -174,12 +179,12 @@
     at = home()
 
     def unfold(low, high):
-        first = iota((HALF, LANES), 1) < 64
+        first = iota((QUART, LANES), 1) < 64
         for j in range(16):
             left, right = low[j], high[j]
             columns = pl.ds((j % 4) * LANES, LANES)
-            rows_out[j // 4, 0:HALF, columns] = jnp.where(first, left, pltpu.roll(right, 64, 1))
-            rows_out[j // 4, HALF:LIVE, columns] = jnp.where(first, pltpu.roll(left, 64, 1), right)
+            rows_out[j // 4, 0:QUART, columns] = jnp.where(first, left, pltpu.roll(right, 64, 1))
+            rows_out[j // 4, QUART:HALF, columns] = jnp.where(first, pltpu.roll(left, 64, 1), right)
 
     @pl.when(at[2] == 0)
     def _():
@@ -189,15 +194,22 @@
     def _():
         unfold(other, own)
 
-    total = jnp.zeros((LIVE, CUT), F32)
+    total = jnp.zeros((HALF, CUT), F32)
     for m, w in enumerate((w0, w1, w2, w3)):
         total = total + dot(rows_out[at[0] ^ m], w[...])
     out[...] = total.astype(BF16)
 
 
-def grads_body(mine, theirs, bias, cot, seg, segt, grad_out, x0, x1, x2, x3):
-    at = home()
-    logits = mine[...].astype(F32) + theirs[...].astype(F32) + bias[pl.ds(at[0], 1), :]
+def grads_body(mine_a, mine_b, theirs_a, theirs_b, bias, cot, seg, segt, grad_out, x0, x1, x2, x3):
+    at = home()
+    logits = jnp.concatenate(
+        [
+            mine_a[...].astype(F32) + theirs_a[...].astype(F32),
+            mine_b[...].astype(F32) + theirs_b[...].astype(F32),
+        ],
+        axis=0,
+    )
+    logits = logits + bias[pl.ds(at[0], 1), :]
     positive = jnp.maximum(logits, 0.0)
     act = jnp.log1p(positive)
     cube = act * act * act
@@ -232,10 +244,12 @@
         out[16:32, :] = tail
 
 
-def weight_grad_body(rows, grad, x0, x1, x2, x3, o0, o1, o2, o3):
+def weight_grad_body(rows_a, rows_b, grad, x0, x1, x2, x3, o0, o1, o2, o3):
     at = home()
     for m, (extra, out) in enumerate(zip((x0, x1, x2, x3), (o0, o1, o2, o3))):
-        out[0:BLOCK, :] = dot(rows[at[0] ^ m], grad[...], ((0,), (0,))).astype(BF16)
+        total = dot(rows_a[at[0] ^ m], grad[0:HALF, :], ((0,), (0,)))
+        total = total + dot(rows_b[at[0] ^ m], grad[HALF:LIVE, :], ((0,), (0,)))
+        out[0:BLOCK, :] = total.astype(BF16)
         out[BLOCK : BLOCK + EXTRA, :] = extra[...]
 
 
@@ -337,14 +351,12 @@
 
     packets = pack(lengths, hidden, rep_cotangent)
     got = trade(packets, ("zp", "zq"))
-    rows, cot, lens = call(
+    rows_a, rows_b, cot, lens = call(
         compact_body,
-        [shape((16, HALF, LANES)), shape((SEQS, CUT), F32), shape((SEQS, LANES), F32)],
+        [shape((16, QUART, LANES))] * 2 + [shape((SEQS, CUT), F32), shape((SEQS, LANES), F32)],
         [got],
         name="compact",
     )
-    own = trade(rows, ("y", "x"))
-    other = swap(own, "c", 2, 1)
     seg, segt, spread = call(
         tables_body,
         [shape((SEQS, LIVE)), shape((LIVE, LANES)), shape((TOKENS, LIVE))],
@@ -353,28 +365,34 @@
         moved=2_000_000,
         name="tables",
     )
-    mine, all_rows = call(
-        logits_body,
-        [shape((LIVE, CUT)), shape((4, LIVE, BLOCK))],
-        [own, other, *w],
-        2 * LIVE * 2048 * CUT,
-        4 << 20,
-        name="logits",
-    )
-    theirs = swap(mine, "zp", 2, 1)
+    mine, theirs, kept = [], [], []
+    for part, rows in (("a", rows_a), ("b", rows_b)):
+        own = trade(rows, ("y", "x"))
+        other = swap(own, "c", 2, 1)
+        logits, whole_rows = call(
+            logits_body,
+            [shape((HALF, CUT)), pltpu.HBM((4, HALF, BLOCK), BF16)],
+            [own, other, *w],
+            2 * HALF * 2048 * CUT,
+            3 << 20,
+            name=f"logits_{part}",
+        )
+        mine.append(logits)
+        kept.append(whole_rows)
+        theirs.append(swap(logits, "zp", 2, 1))
     halves = call(halves_body, shape((4, CUT, CUT)), w, 0, 1 << 20, name="halves")
     halves = swap(halves, "c", 2, 1)
     grad, *extra = call(
         grads_body,
         [shape((LIVE, CUT))] + [shape((EXTRA, CUT))] * 4,
-        [mine, theirs, head_bias.reshape(4, CUT), cot, seg, segt],
+        [*mine, *theirs, head_bias.reshape(4, CUT), cot, seg, segt],
         name="grads",
     )
     partner = swap(grad, "c", 2, 1)
     pieces = call(
         weight_grad_body,
         [shape((BLOCK + EXTRA, CUT))] * 4,
-        [all_rows, grad, *extra],
+        [*kept, grad, *extra],
         2 * LIVE * 2048 * CUT,
         4 << 20,
         name="weight_grad",

time: 209 us -> 224 us (1.072)
  the two profiles are of different devices: /device:TPU:64 before, /device:TPU:32 now
where the time goes in v4:
time: 224 us; the launch traced here: 223 us
  blocking collectives  76.5 us (34%)
  waiting for transfers between devices  68.6 us (31%)
  starting transfers between devices  54.2 us (24%)
  Pallas kernels  19.6 us (9%)
  local copies, waits for them, and re-layouts  2.93 us (1%)
    all_to_all x3, blocking collectives, trade(): return lax.all_to_all(value, axes, 0, 0, tiled=True)  76.5 us
    ppermute x12, waiting for transfers between devices, swap(): return lax.ppermute(value, axis, [(i, i ^ m) for i in range(size)])  59.7 us
    ppermute x12, starting transfers between devices, swap(): return lax.ppermute(value, axis, [(i, i ^ m) for i in range(size)])  35.8 us
    all_to_all x2, starting transfers between devices, trade(): return lax.all_to_all(value, axes, 0, 0, tiled=True)  18.3 us
    pallas_call x11, Pallas kernels, kernel(): pl.pallas_call(body, out_shape=jax.tree.map(lambda o: place(o.shape, o.dt...  16.7 us
    all_to_all x2, waiting for transfers between devices, trade(): return lax.all_to_all(value, axes, 0, 0, tiled=True)  8.88 us
  transfers between devices with their start and end apart: 14, of which 10 were waited for; matrix products, arithmetic and copies ran while one was open for 0% of the time, Pallas kernels for 5%

profile of v4, /device:TPU:32, one launch (start us, length us, event | category | flops | bytes accessed | tf_op | source)
XLA Modules:
  0.0 222.6 jit_solution(9019426542228651607)
XLA Ops:
  2.2 26.0 %all_to_all.25.got = bf16[8,96,128]{2,1,0:T(8,128)(2,1)S(1)} all-to-all(bf16[8,96,128]{2,1,0:T(8,128)(2,1)S(1)} %packet.1), channel_id=1, replica_groups=mesh['zh'=2,'y'=4,'c'=2,'zp'=2,'zq'=4,'x'=4] {'zp','zq'}, dimensions={0} | all-to-all | bytes 393216 | tf_op jit(solution)/shard_map/all_to_all | solution.py:347
  29.7 17.7 %all_to_all.26.own = bf16[16,160,128]{2,1,0:T(8,128)(2,1)S(1)} all-to-all(bf16[16,160,128]{2,1,0:T(8,128)(2,1)S(1)} %get-tuple-element.39), channel_id=1, replica_groups=mesh['zh'=2,'y'=4,'c'=2,'zp'=2,'zq'=4,'x'=4] {'y','x'}, dimensions={0} | all-to-all | bytes 1310720 | tf_op jit(solution)/shard_map/all_to_all | solution.py:347
  47.4 3.6 %all-to-all-start.1 = ((bf16[16,160,128]{2,1,0:T(8,128)(2,1)}), bf16[16,160,128]{2,1,0:T(8,128)(2,1)S(1)}, u32[]{:S(2)}, u32[]{:S(2)}) async-start(bf16[16,160,128]{2,1,0:T(8,128)(2,1)} %get-tuple-element.33), calls=%async_computation.1 | async-start | bytes 1310720 | tf_op jit(solution)/shard_map/all_to_all | solution.py:347
  52.9 8.9 %all-to-all-done.1.own = bf16[16,160,128]{2,1,0:T(8,128)(2,1)S(1)} async-done(((bf16[16,160,128]{2,1,0:T(8,128)(2,1)}), bf16[16,160,128]{2,1,0:T(8,128)(2,1)S(1)}, u32[]{:S(2)}, u32[]{:S(2)}) %all-to-all-start.1) | async-done | bytes 655392 | tf_op jit(solution)/shard_map/all_to_all | solution.py:347
  65.0 2.2 collective-permute-start.1
  67.1 3.9 %collective-permute-start.2 = (bf16[512,256]{1,0:T(8,128)(2,1)S(1)}, bf16[512,256]{1,0:T(8,128)(2,1)S(1)}, u32[]{:S(2)}, u32[]{:S(2)}) collective-permute-start(bf16[512,256]{1,0:T(8,128)(2,1)S(1)} %get-tuple-element.36), channel_id=1, source_target_pairs={{0,8},{4,12},{8,0},{12,4},{1,9},{5,13},{9,1},{13,5},{2,10},{6,14},... | collective-permute-start | bytes 786440 | tf_op jit(solution)/shard_map/ppermute | solution.py:344
  71.0 3.2 %collective-permute-start.3 = (bf16[512,256]{1,0:T(8,128)(2,1)S(1)}, bf16[512,256]{1,0:T(8,128)(2,1)S(1)}, u32[]{:S(2)}, u32[]{:S(2)}) collective-permute-start(bf16[512,256]{1,0:T(8,128)(2,1)S(1)} %get-tuple-element.37), channel_id=1, source_target_pairs={{0,12},{4,8},{8,4},{12,0},{1,13},{5,9},{9,5},{13,1},{2,14},{6,10},... | collective-permute-start | bytes 786440 | tf_op jit(solution)/shard_map/ppermute | solution.py:344
  74.2 1.9 collective-permute-done.1.w1
  76.1 12.8 %collective-permute-done.2.w2 = bf16[512,256]{1,0:T(8,128)(2,1)S(1)} collective-permute-done((bf16[512,256]{1,0:T(8,128)(2,1)S(1)}, bf16[512,256]{1,0:T(8,128)(2,1)S(1)}, u32[]{:S(2)}, u32[]{:S(2)}) %collective-permute-start.2) | collective-permute-done | bytes 262176 | tf_op jit(solution)/shard_map/ppermute | solution.py:344
  89.0 6.6 %collective-permute-done.3.w3 = bf16[512,256]{1,0:T(8,128)(2,1)S(1)} collective-permute-done((bf16[512,256]{1,0:T(8,128)(2,1)S(1)}, bf16[512,256]{1,0:T(8,128)(2,1)S(1)}, u32[]{:S(2)}, u32[]{:S(2)}) %collective-permute-start.3) | collective-permute-done | bytes 262176 | tf_op jit(solution)/shard_map/ppermute | solution.py:344
  99.4 5.0 %collective-permute-start.6 = (bf16[320,256]{1,0:T(8,128)(2,1)}, bf16[320,256]{1,0:T(8,128)(2,1)S(1)}, u32[]{:S(2)}, u32[]{:S(2)}) collective-permute-start(bf16[320,256]{1,0:T(8,128)(2,1)} %get-tuple-element.42.mine_b), channel_id=1, source_target_pairs={{0,16},{16,0},{1,17},{17,1},{2,18},{18,2},{3,19},{19,3},{4,20},{20... | collective-permute-start | bytes 491528 | tf_op jit(solution)/shard_map/ppermute | solution.py:344
  106.0 4.7 %collective-permute-start.5 = (bf16[320,256]{1,0:T(8,128)(2,1)S(1)}, bf16[320,256]{1,0:T(8,128)(2,1)S(1)}, u32[]{:S(2)}, u32[]{:S(2)}) collective-permute-start(bf16[320,256]{1,0:T(8,128)(2,1)S(1)} %get-tuple-element.41.mine_a), channel_id=1, source_target_pairs={{0,16},{16,0},{1,17},{17,1},{2,18},{18,2},{3,19},{19,3},{4,20},{20... | collective-permute-start | bytes 491528 | tf_op jit(solution)/shard_map/ppermute | solution.py:344
  112.3 10.5 %collective-permute-done.6.theirs_b = bf16[320,256]{1,0:T(8,128)(2,1)S(1)} collective-permute-done((bf16[320,256]{1,0:T(8,128)(2,1)}, bf16[320,256]{1,0:T(8,128)(2,1)S(1)}, u32[]{:S(2)}, u32[]{:S(2)}) %collective-permute-start.6) | collective-permute-done | bytes 163872 | tf_op jit(solution)/shard_map/ppermute | solution.py:344
  122.8 3.2 %collective-permute-done.5.theirs_a = bf16[320,256]{1,0:T(8,128)(2,1)S(1)} collective-permute-done((bf16[320,256]{1,0:T(8,128)(2,1)S(1)}, bf16[320,256]{1,0:T(8,128)(2,1)S(1)}, u32[]{:S(2)}, u32[]{:S(2)}) %collective-permute-start.5) | collective-permute-done | bytes 163872 | tf_op jit(solution)/shard_map/ppermute | solution.py:344
  126.9 2.1 shard_map.96
  132.5 4.6 %shard_map.100 = bf16[1024,1024]{1,0:T(8,128)(2,1)} custom-call(bf16[1024,640]{1,0:T(8,128)(2,1)S(1)} %get-tuple-element.60.spread, bf16[640,256]{1,0:T(8,128)(2,1)S(1)} %get-tuple-element.47.grad, bf16[640,256]{1,0:T(8,128)(2,1)S(1)} %collective-permute-done.10.partner, bf16[512,256]{1,0:T(8,128)(2,1)S(1)} %get-tuple-element.34.w0, ...), custom_call_target="tpu_custom_call" | custom-call | flops 1073741824 | bytes 4194304 | tf_op jit(solution)/shard_map/pallas_call | solution.py:40
  137.1 32.8 %all_to_all.27.got = bf16[16,64,1024]{2,1,0:T(8,128)(2,1)S(1)} all-to-all(bf16[16,64,1024]{2,1,0:T(8,128)(2,1)} %bitcast.3), channel_id=1, replica_groups=mesh['zh'=2,'y'=4,'c'=2,'zp'=2,'zq'=4,'x'=4] {'y','x'}, dimensions={0} | all-to-all | bytes 4194304 | tf_op jit(solution)/shard_map/all_to_all | solution.py:347
  170.8 14.7 %all-to-all-start.4 = ((bf16[16,16,256]{2,1,0:T(8,128)(2,1)}), bf16[16,16,256]{2,1,0:T(8,128)(2,1)S(1)}, u32[]{:S(2)}, u32[]{:S(2)}) async-start(bf16[16,16,256]{2,1,0:T(8,128)(2,1)} %shard_map.101), calls=%async_computation.4 | async-start | bytes 262144 | tf_op jit(solution)/shard_map/all_to_all | solution.py:347
  188.2 2.0 collective-permute-start.7
  190.2 4.7 %collective-permute-start.8 = (bf16[544,256]{1,0:T(8,128)(2,1)S(1)}, bf16[544,256]{1,0:T(8,128)(2,1)S(1)}, u32[]{:S(2)}, u32[]{:S(2)}) collective-permute-start(bf16[544,256]{1,0:T(8,128)(2,1)S(1)} %get-tuple-element.54), channel_id=1, source_target_pairs={{0,8},{4,12},{8,0},{12,4},{1,9},{5,13},{9,1},{13,5},{2,10},{6,14},... | collective-permute-start | bytes 835592 | tf_op jit(solution)/shard_map/ppermute | solution.py:344
  194.9 2.5 %collective-permute-start.9 = (bf16[544,256]{1,0:T(8,128)(2,1)S(1)}, bf16[544,256]{1,0:T(8,128)(2,1)S(1)}, u32[]{:S(2)}, u32[]{:S(2)}) collective-permute-start(bf16[544,256]{1,0:T(8,128)(2,1)S(1)} %get-tuple-element.55), channel_id=1, source_target_pairs={{0,12},{4,8},{8,4},{12,0},{1,13},{5,9},{9,5},{13,1},{2,14},{6,10},... | collective-permute-start | bytes 835592 | tf_op jit(solution)/shard_map/ppermute | solution.py:344
  197.4 4.9 %collective-permute-done.7.p1 = bf16[544,256]{1,0:T(8,128)(2,1)S(1)} collective-permute-done((bf16[544,256]{1,0:T(8,128)(2,1)S(1)}, bf16[544,256]{1,0:T(8,128)(2,1)S(1)}, u32[]{:S(2)}, u32[]{:S(2)}) %collective-permute-start.7) | collective-permute-done | bytes 278560 | tf_op jit(solution)/shard_map/ppermute | solution.py:344
  202.3 12.1 %collective-permute-done.8.p2 = bf16[544,256]{1,0:T(8,128)(2,1)S(1)} collective-permute-done((bf16[544,256]{1,0:T(8,128)(2,1)S(1)}, bf16[544,256]{1,0:T(8,128)(2,1)S(1)}, u32[]{:S(2)}, u32[]{:S(2)}) %collective-permute-start.8) | collective-permute-done | bytes 278560 | tf_op jit(solution)/shard_map/ppermute | solution.py:344
  214.4 6.0 %collective-permute-done.9.p3 = bf16[544,256]{1,0:T(8,128)(2,1)S(1)} collective-permute-done((bf16[544,256]{1,0:T(8,128)(2,1)S(1)}, bf16[544,256]{1,0:T(8,128)(2,1)S(1)}, u32[]{:S(2)}, u32[]{:S(2)}) %collective-permute-start.9) | collective-permute-done | bytes 278560 | tf_op jit(solution)/shard_map/ppermute | solution.py:344
  (35 shorter events, 25.1 us)
Async XLA Ops:
  29.7 17.7 %copy-start.2 = (f32[64,256]{1,0:T(8,128)}, f32[64,256]{1,0:T(8,128)S(1)}, u32[]{:S(2)}) copy-start(f32[64,256]{1,0:T(8,128)S(1)} %get-tuple-element.43.cot) | copy-start | bytes 196612
  29.7 17.7 %copy-start.4 = (f32[64,128]{1,0:T(8,128)}, f32[64,128]{1,0:T(8,128)S(1)}, u32[]{:S(2)}) copy-start(f32[64,128]{1,0:T(8,128)S(1)} %get-tuple-element.44.len_ref) | copy-start | bytes 98308
  47.4 14.4 %all-to-all-start.1 = ((bf16[16,160,128]{2,1,0:T(8,128)(2,1)}), bf16[16,160,128]{2,1,0:T(8,128)(2,1)S(1)}, u32[]{:S(2)}, u32[]{:S(2)}) async-start(bf16[16,160,128]{2,1,0:T(8,128)(2,1)} %get-tuple-element.33), calls=%async_computation.1 | async-start | bytes 1310720 | tf_op jit(solution)/shard_map/all_to_all | solution.py:347
  51.0 46.6 %collective-permute-start.4 = (bf16[16,160,128]{2,1,0:T(8,128)(2,1)S(1)}, bf16[16,160,128]{2,1,0:T(8,128)(2,1)S(1)}, u32[]{:S(2)}, u32[]{:S(2)}) collective-permute-start(bf16[16,160,128]{2,1,0:T(8,128)(2,1)S(1)} %all_to_all.26.own), channel_id=1, source_target_pairs={{0,32},{32,0},{1,33},{33,1},{2,34},{34,2},{3,35},{35,3},{4,36},{36... | collective-permute-start | bytes 1966088 | tf_op jit(solution)/shard_map/ppermute | solution.py:344
  61.8 42.6 %collective-permute-start = (bf16[16,160,128]{2,1,0:T(8,128)(2,1)S(1)}, bf16[16,160,128]{2,1,0:T(8,128)(2,1)S(1)}, u32[]{:S(2)}, u32[]{:S(2)}) collective-permute-start(bf16[16,160,128]{2,1,0:T(8,128)(2,1)S(1)} %all-to-all-done.1.own), channel_id=1, source_target_pairs={{0,32},{32,0},{1,33},{33,1},{2,34},{34,2},{3,35},{35,3},{4,36},{36... | collective-permute-start | bytes 1966088 | tf_op jit(solution)/shard_map/ppermute | solution.py:344
  65.0 11.2 %collective-permute-start.1 = (bf16[512,256]{1,0:T(8,128)(2,1)S(1)}, bf16[512,256]{1,0:T(8,128)(2,1)S(1)}, u32[]{:S(2)}, u32[]{:S(2)}) collective-permute-start(bf16[512,256]{1,0:T(8,128)(2,1)S(1)} %get-tuple-element.35), channel_id=1, source_target_pairs={{0,4},{4,0},{8,12},{12,8},{1,5},{5,1},{9,13},{13,9},{2,6},{6,2},{1... | collective-permute-start | bytes 786440 | tf_op jit(solution)/shard_map/ppermute | solution.py:344
  67.1 21.8 %collective-permute-start.2 = (bf16[512,256]{1,0:T(8,128)(2,1)S(1)}, bf16[512,256]{1,0:T(8,128)(2,1)S(1)}, u32[]{:S(2)}, u32[]{:S(2)}) collective-permute-start(bf16[512,256]{1,0:T(8,128)(2,1)S(1)} %get-tuple-element.36), channel_id=1, source_target_pairs={{0,8},{4,12},{8,0},{12,4},{1,9},{5,13},{9,1},{13,5},{2,10},{6,14},... | collective-permute-start | bytes 786440 | tf_op jit(solution)/shard_map/ppermute | solution.py:344
  71.0 24.6 %collective-permute-start.3 = (bf16[512,256]{1,0:T(8,128)(2,1)S(1)}, bf16[512,256]{1,0:T(8,128)(2,1)S(1)}, u32[]{:S(2)}, u32[]{:S(2)}) collective-permute-start(bf16[512,256]{1,0:T(8,128)(2,1)S(1)} %get-tuple-element.37), channel_id=1, source_target_pairs={{0,12},{4,8},{8,4},{12,0},{1,13},{5,9},{9,5},{13,1},{2,14},{6,10},... | collective-permute-start | bytes 786440 | tf_op jit(solution)/shard_map/ppermute | solution.py:344
  95.6 15.1 %copy-start.6 = (f32[1024]{0:T(1024)S(1)}, f32[1024]{0:T(1024)}, u32[]{:S(2)}) copy-start(f32[1024]{0:T(1024)} %param.7) | copy-start | bytes 12292
  95.6 35.3 %collective-permute-start.11 = (bf16[4,256,256]{2,1,0:T(8,128)(2,1)S(1)}, bf16[4,256,256]{2,1,0:T(8,128)(2,1)}, u32[]{:S(2)}, u32[]{:S(2)}) collective-permute-start(bf16[4,256,256]{2,1,0:T(8,128)(2,1)S(1)} %shard_map.99), channel_id=1, source_target_pairs={{0,32},{32,0},{1,33},{33,1},{2,34},{34,2},{3,35},{35,3},{4,36},{36... | collective-permute-start | bytes 1572872 | tf_op jit(solution)/shard_map/ppermute | solution.py:344
  99.4 23.4 %collective-permute-start.6 = (bf16[320,256]{1,0:T(8,128)(2,1)}, bf16[320,256]{1,0:T(8,128)(2,1)S(1)}, u32[]{:S(2)}, u32[]{:S(2)}) collective-permute-start(bf16[320,256]{1,0:T(8,128)(2,1)} %get-tuple-element.42.mine_b), channel_id=1, source_target_pairs={{0,16},{16,0},{1,17},{17,1},{2,18},{18,2},{3,19},{19,3},{4,20},{20... | collective-permute-start | bytes 491528 | tf_op jit(solution)/shard_map/ppermute | solution.py:344
  106.0 20.0 %collective-permute-start.5 = (bf16[320,256]{1,0:T(8,128)(2,1)S(1)}, bf16[320,256]{1,0:T(8,128)(2,1)S(1)}, u32[]{:S(2)}, u32[]{:S(2)}) collective-permute-start(bf16[320,256]{1,0:T(8,128)(2,1)S(1)} %get-tuple-element.41.mine_a), channel_id=1, source_target_pairs={{0,16},{16,0},{1,17},{17,1},{2,18},{18,2},{3,19},{19,3},{4,20},{20... | collective-permute-start | bytes 491528 | tf_op jit(solution)/shard_map/ppermute | solution.py:344
  110.8 0.8 copy-start.5
  126.1 0.8 copy-start.3
  129.0 3.5 %collective-permute-start.10 = (bf16[640,256]{1,0:T(8,128)(2,1)S(1)}, bf16[640,256]{1,0:T(8,128)(2,1)S(1)}, u32[]{:S(2)}, u32[]{:S(2)}) collective-permute-start(bf16[640,256]{1,0:T(8,128)(2,1)S(1)} %get-tuple-element.47.grad), channel_id=1, source_target_pairs={{0,32},{32,0},{1,33},{33,1},{2,34},{34,2},{3,35},{35,3},{4,36},{36... | collective-permute-start | bytes 983048 | tf_op jit(solution)/shard_map/ppermute | solution.py:344
  169.9 15.7 %copy-start = (bf16[4,320,512]{2,1,0:T(8,128)(2,1)S(1)}, bf16[4,320,512]{2,1,0:T(8,128)(2,1)}, u32[]{:S(2)}) copy-start(bf16[4,320,512]{2,1,0:T(8,128)(2,1)} %get-tuple-element.40.rows_b) | copy-start | bytes 3932164
  170.8 51.2 %all-to-all-start.4 = ((bf16[16,16,256]{2,1,0:T(8,128)(2,1)}), bf16[16,16,256]{2,1,0:T(8,128)(2,1)S(1)}, u32[]{:S(2)}, u32[]{:S(2)}) async-start(bf16[16,16,256]{2,1,0:T(8,128)(2,1)} %shard_map.101), calls=%async_computation.4 | async-start | bytes 262144 | tf_op jit(solution)/shard_map/all_to_all | solution.py:347
  185.5 1.3 copy-start.1
  188.2 14.1 %collective-permute-start.7 = (bf16[544,256]{1,0:T(8,128)(2,1)S(1)}, bf16[544,256]{1,0:T(8,128)(2,1)S(1)}, u32[]{:S(2)}, u32[]{:S(2)}) collective-permute-start(bf16[544,256]{1,0:T(8,128)(2,1)S(1)} %get-tuple-element.53), channel_id=1, source_target_pairs={{0,4},{4,0},{8,12},{12,8},{1,5},{5,1},{9,13},{13,9},{2,6},{6,2},{1... | collective-permute-start | bytes 835592 | tf_op jit(solution)/shard_map/ppermute | solution.py:344
  190.2 24.2 %collective-permute-start.8 = (bf16[544,256]{1,0:T(8,128)(2,1)S(1)}, bf16[544,256]{1,0:T(8,128)(2,1)S(1)}, u32[]{:S(2)}, u32[]{:S(2)}) collective-permute-start(bf16[544,256]{1,0:T(8,128)(2,1)S(1)} %get-tuple-element.54), channel_id=1, source_target_pairs={{0,8},{4,12},{8,0},{12,4},{1,9},{5,13},{9,1},{13,5},{2,10},{6,14},... | collective-permute-start | bytes 835592 | tf_op jit(solution)/shard_map/ppermute | solution.py:344
  194.9 25.5 %collective-permute-start.9 = (bf16[544,256]{1,0:T(8,128)(2,1)S(1)}, bf16[544,256]{1,0:T(8,128)(2,1)S(1)}, u32[]{:S(2)}, u32[]{:S(2)}) collective-permute-start(bf16[544,256]{1,0:T(8,128)(2,1)S(1)} %get-tuple-element.55), channel_id=1, source_target_pairs={{0,12},{4,8},{8,4},{12,0},{1,13},{5,9},{9,5},{13,1},{2,14},{6,10},... | collective-permute-start | bytes 835592 | tf_op jit(solution)/shard_map/ppermute | solution.py:344

commit v5 on v4

--- a/solution.py
+++ b/solution.py
@@ -47,7 +47,7 @@
     )(*ins)
 
 
-KEEP = ("compact", "grads", "halves", "plane", "tables")
+KEEP = ("early", "compact", "grads", "halves", "plane", "tables")
 LEAVE = ("input",)
 FREE = ("weight_grad", "unpack")
 
@@ -200,21 +200,25 @@
     out[...] = total.astype(BF16)
 
 
-def grads_body(mine_a, mine_b, theirs_a, theirs_b, bias, cot, seg, segt, grad_out, x0, x1, x2, x3):
-    at = home()
-    logits = jnp.concatenate(
-        [
-            mine_a[...].astype(F32) + theirs_a[...].astype(F32),
-            mine_b[...].astype(F32) + theirs_b[...].astype(F32),
-        ],
-        axis=0,
-    )
-    logits = logits + bias[pl.ds(at[0], 1), :]
+def activate(mine, theirs, bias, seg):
+    logits = mine[...].astype(F32) + theirs[...].astype(F32) + bias[pl.ds(home()[0], 1), :]
     positive = jnp.maximum(logits, 0.0)
     act = jnp.log1p(positive)
     cube = act * act * act
     high, low = split(cube * act)
-    total = 1.0 + (dot(seg[...], high) + dot(seg[...], low))
+    return cube / (1.0 + positive), dot(seg, high) + dot(seg, low)
+
+
+def early_body(mine, theirs, bias, seg, slope_out, sum_out):
+    slope, total = activate(mine, theirs, bias, seg[...][:, 0:HALF])
+    slope_out[...] = slope
+    sum_out[...] = total
+
+
+def grads_body(mine, theirs, slope_a, sum_a, bias, cot, seg, segt, grad_out, x0, x1, x2, x3):
+    at = home()
+    slope_b, sum_b = activate(mine, theirs, bias, seg[...][:, HALF:LIVE])
+    total = 1.0 + (sum_a[...] + sum_b)
     second = jnp.sqrt(total)
     fourth = jnp.sqrt(second)
     pooled = fourth - 1.0
@@ -224,7 +228,7 @@
     high, low = split(pull)
     spread = dot(segt[...], jnp.concatenate([high, pad], axis=0))
     spread = spread + dot(segt[...], jnp.concatenate([low, pad], axis=0))
-    grad = spread * (cube / (1.0 + positive))
+    grad = spread * jnp.concatenate([slope_a[...], slope_b], axis=0)
     bias_grad = jnp.sum(grad, axis=0, keepdims=True)
     grad_out[...] = grad.astype(BF16)
     m_high, m_low = split(mean)
@@ -382,10 +386,17 @@
         theirs.append(swap(logits, "zp", 2, 1))
     halves = call(halves_body, shape((4, CUT, CUT)), w, 0, 1 << 20, name="halves")
     halves = swap(halves, "c", 2, 1)
+    bias = head_bias.reshape(4, CUT)
+    early = call(
+        early_body,
+        [shape((HALF, CUT), F32), shape((SEQS, CUT), F32)],
+        [mine[0], theirs[0], bias, seg],
+        name="early",
+    )
     grad, *extra = call(
         grads_body,
         [shape((LIVE, CUT))] + [shape((EXTRA, CUT))] * 4,
-        [*mine, *theirs, head_bias.reshape(4, CUT), cot, seg, segt],
+        [mine[1], theirs[1], *early, bias, cot, seg, segt],
         name="grads",
     )
     partner = swap(grad, "c", 2, 1)

time: 224 us -> 223 us (level)
    pallas_call x11 -> x12, Pallas kernels: 16.7 us -> 16.9 us  [kernel(): pl.pallas_call(body, out_shape=jax.tree.map(lambda o: place(o.shape, o.dt...]
where the time goes in v5:
time: 223 us; the launch traced here: 221 us
  blocking collectives  76.5 us (34%)
  waiting for transfers between devices  67.3 us (30%)
  starting transfers between devices  54.2 us (24%)
  Pallas kernels  19.7 us (9%)
  local copies, waits for them, and re-layouts  2.93 us (1%)
    all_to_all x3, blocking collectives, trade(): return lax.all_to_all(value, axes, 0, 0, tiled=True)  76.5 us
    ppermute x12, waiting for transfers between devices, swap(): return lax.ppermute(value, axis, [(i, i ^ m) for i in range(size)])  58.5 us
    ppermute x12, starting transfers between devices, swap(): return lax.ppermute(value, axis, [(i, i ^ m) for i in range(size)])  35.8 us
    all_to_all x2, starting transfers between devices, trade(): return lax.all_to_all(value, axes, 0, 0, tiled=True)  18.3 us
    pallas_call x12, Pallas kernels, kernel(): pl.pallas_call(body, out_shape=jax.tree.map(lambda o: place(o.shape, o.dt...  16.9 us
    all_to_all x2, waiting for transfers between devices, trade(): return lax.all_to_all(value, axes, 0, 0, tiled=True)  8.88 us
  transfers between devices with their start and end apart: 14, of which 10 were waited for; matrix products, arithmetic and copies ran while one was open for 0% of the time, Pallas kernels for 5%

profile of v5, /device:TPU:32, one launch (start us, length us, event | category | flops | bytes accessed | tf_op | source)
XLA Modules:
  0.0 221.4 jit_solution(4403546936977209012)
XLA Ops:
  2.2 26.0 %all_to_all.25.got = bf16[8,96,128]{2,1,0:T(8,128)(2,1)S(1)} all-to-all(bf16[8,96,128]{2,1,0:T(8,128)(2,1)S(1)} %packet.1), channel_id=1, replica_groups=mesh['zh'=2,'y'=4,'c'=2,'zp'=2,'zq'=4,'x'=4] {'zp','zq'}, dimensions={0} | all-to-all | bytes 393216 | tf_op jit(solution)/shard_map/all_to_all | solution.py:351
  29.8 17.7 %all_to_all.26.own = bf16[16,160,128]{2,1,0:T(8,128)(2,1)S(1)} all-to-all(bf16[16,160,128]{2,1,0:T(8,128)(2,1)S(1)} %get-tuple-element.35), channel_id=1, replica_groups=mesh['zh'=2,'y'=4,'c'=2,'zp'=2,'zq'=4,'x'=4] {'y','x'}, dimensions={0} | all-to-all | bytes 1310720 | tf_op jit(solution)/shard_map/all_to_all | solution.py:351
  47.5 3.6 %all-to-all-start.2 = ((bf16[16,160,128]{2,1,0:T(8,128)(2,1)}), bf16[16,160,128]{2,1,0:T(8,128)(2,1)S(1)}, u32[]{:S(2)}, u32[]{:S(2)}) async-start(bf16[16,160,128]{2,1,0:T(8,128)(2,1)} %get-tuple-element.41), calls=%async_computation.2 | async-start | bytes 1310720 | tf_op jit(solution)/shard_map/all_to_all | solution.py:351
  53.0 8.9 %all-to-all-done.2.own = bf16[16,160,128]{2,1,0:T(8,128)(2,1)S(1)} async-done(((bf16[16,160,128]{2,1,0:T(8,128)(2,1)}), bf16[16,160,128]{2,1,0:T(8,128)(2,1)S(1)}, u32[]{:S(2)}, u32[]{:S(2)}) %all-to-all-start.2) | async-done | bytes 655392 | tf_op jit(solution)/shard_map/all_to_all | solution.py:351
  65.1 2.2 collective-permute-start.1
  67.2 3.9 %collective-permute-start.2 = (bf16[512,256]{1,0:T(8,128)(2,1)S(1)}, bf16[512,256]{1,0:T(8,128)(2,1)S(1)}, u32[]{:S(2)}, u32[]{:S(2)}) collective-permute-start(bf16[512,256]{1,0:T(8,128)(2,1)S(1)} %get-tuple-element.38), channel_id=1, source_target_pairs={{0,8},{4,12},{8,0},{12,4},{1,9},{5,13},{9,1},{13,5},{2,10},{6,14},... | collective-permute-start | bytes 786440 | tf_op jit(solution)/shard_map/ppermute | solution.py:348
  71.1 3.2 %collective-permute-start.3 = (bf16[512,256]{1,0:T(8,128)(2,1)S(1)}, bf16[512,256]{1,0:T(8,128)(2,1)S(1)}, u32[]{:S(2)}, u32[]{:S(2)}) collective-permute-start(bf16[512,256]{1,0:T(8,128)(2,1)S(1)} %get-tuple-element.39), channel_id=1, source_target_pairs={{0,12},{4,8},{8,4},{12,0},{1,13},{5,9},{9,5},{13,1},{2,14},{6,10},... | collective-permute-start | bytes 786440 | tf_op jit(solution)/shard_map/ppermute | solution.py:348
  74.3 1.9 collective-permute-done.1.w1
  76.2 12.8 %collective-permute-done.2.w2 = bf16[512,256]{1,0:T(8,128)(2,1)S(1)} collective-permute-done((bf16[512,256]{1,0:T(8,128)(2,1)S(1)}, bf16[512,256]{1,0:T(8,128)(2,1)S(1)}, u32[]{:S(2)}, u32[]{:S(2)}) %collective-permute-start.2) | collective-permute-done | bytes 262176 | tf_op jit(solution)/shard_map/ppermute | solution.py:348
  89.1 6.6 %collective-permute-done.3.w3 = bf16[512,256]{1,0:T(8,128)(2,1)S(1)} collective-permute-done((bf16[512,256]{1,0:T(8,128)(2,1)S(1)}, bf16[512,256]{1,0:T(8,128)(2,1)S(1)}, u32[]{:S(2)}, u32[]{:S(2)}) %collective-permute-start.3) | collective-permute-done | bytes 262176 | tf_op jit(solution)/shard_map/ppermute | solution.py:348
  95.7 1.9 collective-permute-start.11
  99.5 5.0 %collective-permute-start.6 = (bf16[320,256]{1,0:T(8,128)(2,1)}, bf16[320,256]{1,0:T(8,128)(2,1)S(1)}, u32[]{:S(2)}, u32[]{:S(2)}) collective-permute-start(bf16[320,256]{1,0:T(8,128)(2,1)} %get-tuple-element.44.mine), channel_id=1, source_target_pairs={{0,16},{16,0},{1,17},{17,1},{2,18},{18,2},{3,19},{19,3},{4,20},{20... | collective-permute-start | bytes 491528 | tf_op jit(solution)/shard_map/ppermute | solution.py:348
  106.1 4.7 %collective-permute-start.5 = (bf16[320,256]{1,0:T(8,128)(2,1)S(1)}, bf16[320,256]{1,0:T(8,128)(2,1)S(1)}, u32[]{:S(2)}, u32[]{:S(2)}) collective-permute-start(bf16[320,256]{1,0:T(8,128)(2,1)S(1)} %get-tuple-element.43.mine), channel_id=1, source_target_pairs={{0,16},{16,0},{1,17},{17,1},{2,18},{18,2},{3,19},{19,3},{4,20},{20... | collective-permute-start | bytes 491528 | tf_op jit(solution)/shard_map/ppermute | solution.py:348
  112.4 10.5 %collective-permute-done.6.theirs = bf16[320,256]{1,0:T(8,128)(2,1)S(1)} collective-permute-done((bf16[320,256]{1,0:T(8,128)(2,1)}, bf16[320,256]{1,0:T(8,128)(2,1)S(1)}, u32[]{:S(2)}, u32[]{:S(2)}) %collective-permute-start.6) | collective-permute-done | bytes 163872 | tf_op jit(solution)/shard_map/ppermute | solution.py:348
  127.8 1.9 collective-permute-start.10
  131.4 4.6 %shard_map.101 = bf16[1024,1024]{1,0:T(8,128)(2,1)} custom-call(bf16[1024,640]{1,0:T(8,128)(2,1)S(1)} %get-tuple-element.64.spread, bf16[640,256]{1,0:T(8,128)(2,1)S(1)} %get-tuple-element.51.grad, bf16[640,256]{1,0:T(8,128)(2,1)S(1)} %collective-permute-done.10.partner, bf16[512,256]{1,0:T(8,128)(2,1)S(1)} %get-tuple-element.36.w0, ...), custom_call_target="tpu_custom_call" | custom-call | flops 1073741824 | bytes 4194304 | tf_op jit(solution)/shard_map/pallas_call | solution.py:40
  135.9 32.8 %all_to_all.27.got = bf16[16,64,1024]{2,1,0:T(8,128)(2,1)S(1)} all-to-all(bf16[16,64,1024]{2,1,0:T(8,128)(2,1)} %bitcast.3), channel_id=1, replica_groups=mesh['zh'=2,'y'=4,'c'=2,'zp'=2,'zq'=4,'x'=4] {'y','x'}, dimensions={0} | all-to-all | bytes 4194304 | tf_op jit(solution)/shard_map/all_to_all | solution.py:351
  169.6 14.7 %all-to-all-start.4 = ((bf16[16,16,256]{2,1,0:T(8,128)(2,1)}), bf16[16,16,256]{2,1,0:T(8,128)(2,1)S(1)}, u32[]{:S(2)}, u32[]{:S(2)}) async-start(bf16[16,16,256]{2,1,0:T(8,128)(2,1)} %shard_map.102), calls=%async_computation.4 | async-start | bytes 262144 | tf_op jit(solution)/shard_map/all_to_all | solution.py:351
  187.0 2.0 collective-permute-start.7
  189.0 4.7 %collective-permute-start.8 = (bf16[544,256]{1,0:T(8,128)(2,1)S(1)}, bf16[544,256]{1,0:T(8,128)(2,1)S(1)}, u32[]{:S(2)}, u32[]{:S(2)}) collective-permute-start(bf16[544,256]{1,0:T(8,128)(2,1)S(1)} %get-tuple-element.58), channel_id=1, source_target_pairs={{0,8},{4,12},{8,0},{12,4},{1,9},{5,13},{9,1},{13,5},{2,10},{6,14},... | collective-permute-start | bytes 835592 | tf_op jit(solution)/shard_map/ppermute | solution.py:348
  193.8 2.5 %collective-permute-start.9 = (bf16[544,256]{1,0:T(8,128)(2,1)S(1)}, bf16[544,256]{1,0:T(8,128)(2,1)S(1)}, u32[]{:S(2)}, u32[]{:S(2)}) collective-permute-start(bf16[544,256]{1,0:T(8,128)(2,1)S(1)} %get-tuple-element.59), channel_id=1, source_target_pairs={{0,12},{4,8},{8,4},{12,0},{1,13},{5,9},{9,5},{13,1},{2,14},{6,10},... | collective-permute-start | bytes 835592 | tf_op jit(solution)/shard_map/ppermute | solution.py:348
  196.3 4.9 %collective-permute-done.7.p1 = bf16[544,256]{1,0:T(8,128)(2,1)S(1)} collective-permute-done((bf16[544,256]{1,0:T(8,128)(2,1)S(1)}, bf16[544,256]{1,0:T(8,128)(2,1)S(1)}, u32[]{:S(2)}, u32[]{:S(2)}) %collective-permute-start.7) | collective-permute-done | bytes 278560 | tf_op jit(solution)/shard_map/ppermute | solution.py:348
  201.2 12.1 %collective-permute-done.8.p2 = bf16[544,256]{1,0:T(8,128)(2,1)S(1)} collective-permute-done((bf16[544,256]{1,0:T(8,128)(2,1)S(1)}, bf16[544,256]{1,0:T(8,128)(2,1)S(1)}, u32[]{:S(2)}, u32[]{:S(2)}) %collective-permute-start.8) | collective-permute-done | bytes 278560 | tf_op jit(solution)/shard_map/ppermute | solution.py:348
  213.3 6.0 %collective-permute-done.9.p3 = bf16[544,256]{1,0:T(8,128)(2,1)S(1)} collective-permute-done((bf16[544,256]{1,0:T(8,128)(2,1)S(1)}, bf16[544,256]{1,0:T(8,128)(2,1)S(1)}, u32[]{:S(2)}, u32[]{:S(2)}) %collective-permute-start.9) | collective-permute-done | bytes 278560 | tf_op jit(solution)/shard_map/ppermute | solution.py:348
  (36 shorter events, 25.4 us)
Async XLA Ops:
  29.8 17.7 %copy-start.2 = (f32[64,256]{1,0:T(8,128)}, f32[64,256]{1,0:T(8,128)S(1)}, u32[]{:S(2)}) copy-start(f32[64,256]{1,0:T(8,128)S(1)} %get-tuple-element.49.cot) | copy-start | bytes 196612
  29.8 17.7 %copy-start.4 = (f32[64,128]{1,0:T(8,128)}, f32[64,128]{1,0:T(8,128)S(1)}, u32[]{:S(2)}) copy-start(f32[64,128]{1,0:T(8,128)S(1)} %get-tuple-element.45.len_ref) | copy-start | bytes 98308
  47.5 14.4 %all-to-all-start.2 = ((bf16[16,160,128]{2,1,0:T(8,128)(2,1)}), bf16[16,160,128]{2,1,0:T(8,128)(2,1)S(1)}, u32[]{:S(2)}, u32[]{:S(2)}) async-start(bf16[16,160,128]{2,1,0:T(8,128)(2,1)} %get-tuple-element.41), calls=%async_computation.2 | async-start | bytes 1310720 | tf_op jit(solution)/shard_map/all_to_all | solution.py:351
  51.1 46.6 %collective-permute-start = (bf16[16,160,128]{2,1,0:T(8,128)(2,1)S(1)}, bf16[16,160,128]{2,1,0:T(8,128)(2,1)S(1)}, u32[]{:S(2)}, u32[]{:S(2)}) collective-permute-start(bf16[16,160,128]{2,1,0:T(8,128)(2,1)S(1)} %all_to_all.26.own), channel_id=1, source_target_pairs={{0,32},{32,0},{1,33},{33,1},{2,34},{34,2},{3,35},{35,3},{4,36},{36... | collective-permute-start | bytes 1966088 | tf_op jit(solution)/shard_map/ppermute | solution.py:348
  61.9 42.6 %collective-permute-start.4 = (bf16[16,160,128]{2,1,0:T(8,128)(2,1)S(1)}, bf16[16,160,128]{2,1,0:T(8,128)(2,1)S(1)}, u32[]{:S(2)}, u32[]{:S(2)}) collective-permute-start(bf16[16,160,128]{2,1,0:T(8,128)(2,1)S(1)} %all-to-all-done.2.own), channel_id=1, source_target_pairs={{0,32},{32,0},{1,33},{33,1},{2,34},{34,2},{3,35},{35,3},{4,36},{36... | collective-permute-start | bytes 1966088 | tf_op jit(solution)/shard_map/ppermute | solution.py:348
  65.1 11.2 %collective-permute-start.1 = (bf16[512,256]{1,0:T(8,128)(2,1)S(1)}, bf16[512,256]{1,0:T(8,128)(2,1)S(1)}, u32[]{:S(2)}, u32[]{:S(2)}) collective-permute-start(bf16[512,256]{1,0:T(8,128)(2,1)S(1)} %get-tuple-element.37), channel_id=1, source_target_pairs={{0,4},{4,0},{8,12},{12,8},{1,5},{5,1},{9,13},{13,9},{2,6},{6,2},{1... | collective-permute-start | bytes 786440 | tf_op jit(solution)/shard_map/ppermute | solution.py:348
  67.2 21.8 %collective-permute-start.2 = (bf16[512,256]{1,0:T(8,128)(2,1)S(1)}, bf16[512,256]{1,0:T(8,128)(2,1)S(1)}, u32[]{:S(2)}, u32[]{:S(2)}) collective-permute-start(bf16[512,256]{1,0:T(8,128)(2,1)S(1)} %get-tuple-element.38), channel_id=1, source_target_pairs={{0,8},{4,12},{8,0},{12,4},{1,9},{5,13},{9,1},{13,5},{2,10},{6,14},... | collective-permute-start | bytes 786440 | tf_op jit(solution)/shard_map/ppermute | solution.py:348
  71.1 24.6 %collective-permute-start.3 = (bf16[512,256]{1,0:T(8,128)(2,1)S(1)}, bf16[512,256]{1,0:T(8,128)(2,1)S(1)}, u32[]{:S(2)}, u32[]{:S(2)}) collective-permute-start(bf16[512,256]{1,0:T(8,128)(2,1)S(1)} %get-tuple-element.39), channel_id=1, source_target_pairs={{0,12},{4,8},{8,4},{12,0},{1,13},{5,9},{9,5},{13,1},{2,14},{6,10},... | collective-permute-start | bytes 786440 | tf_op jit(solution)/shard_map/ppermute | solution.py:348
  95.7 15.1 %copy-start.6 = (f32[1024]{0:T(1024)S(1)}, f32[1024]{0:T(1024)}, u32[]{:S(2)}) copy-start(f32[1024]{0:T(1024)} %param.7) | copy-start | bytes 12292
  95.7 34.1 %collective-permute-start.11 = (bf16[4,256,256]{2,1,0:T(8,128)(2,1)S(1)}, bf16[4,256,256]{2,1,0:T(8,128)(2,1)}, u32[]{:S(2)}, u32[]{:S(2)}) collective-permute-start(bf16[4,256,256]{2,1,0:T(8,128)(2,1)S(1)} %shard_map.100), channel_id=1, source_target_pairs={{0,32},{32,0},{1,33},{33,1},{2,34},{34,2},{3,35},{35,3},{4,36},{36... | collective-permute-start | bytes 1572872 | tf_op jit(solution)/shard_map/ppermute | solution.py:348
  99.5 23.4 %collective-permute-start.6 = (bf16[320,256]{1,0:T(8,128)(2,1)}, bf16[320,256]{1,0:T(8,128)(2,1)S(1)}, u32[]{:S(2)}, u32[]{:S(2)}) collective-permute-start(bf16[320,256]{1,0:T(8,128)(2,1)} %get-tuple-element.44.mine), channel_id=1, source_target_pairs={{0,16},{16,0},{1,17},{17,1},{2,18},{18,2},{3,19},{19,3},{4,20},{20... | collective-permute-start | bytes 491528 | tf_op jit(solution)/shard_map/ppermute | solution.py:348
  106.1 20.1 %collective-permute-start.5 = (bf16[320,256]{1,0:T(8,128)(2,1)S(1)}, bf16[320,256]{1,0:T(8,128)(2,1)S(1)}, u32[]{:S(2)}, u32[]{:S(2)}) collective-permute-start(bf16[320,256]{1,0:T(8,128)(2,1)S(1)} %get-tuple-element.43.mine), channel_id=1, source_target_pairs={{0,16},{16,0},{1,17},{17,1},{2,18},{18,2},{3,19},{19,3},{4,20},{20... | collective-permute-start | bytes 491528 | tf_op jit(solution)/shard_map/ppermute | solution.py:348
  110.8 0.8 copy-start.5
  126.1 0.8 copy-start.3
  127.8 3.5 %collective-permute-start.10 = (bf16[640,256]{1,0:T(8,128)(2,1)S(1)}, bf16[640,256]{1,0:T(8,128)(2,1)S(1)}, u32[]{:S(2)}, u32[]{:S(2)}) collective-permute-start(bf16[640,256]{1,0:T(8,128)(2,1)S(1)} %get-tuple-element.51.grad), channel_id=1, source_target_pairs={{0,32},{32,0},{1,33},{33,1},{2,34},{34,2},{3,35},{35,3},{4,36},{36... | collective-permute-start | bytes 983048 | tf_op jit(solution)/shard_map/ppermute | solution.py:348
  168.7 15.7 %copy-start = (bf16[4,320,512]{2,1,0:T(8,128)(2,1)S(1)}, bf16[4,320,512]{2,1,0:T(8,128)(2,1)}, u32[]{:S(2)}) copy-start(bf16[4,320,512]{2,1,0:T(8,128)(2,1)} %get-tuple-element.40.rows_a) | copy-start | bytes 3932164
  169.6 51.2 %all-to-all-start.4 = ((bf16[16,16,256]{2,1,0:T(8,128)(2,1)}), bf16[16,16,256]{2,1,0:T(8,128)(2,1)S(1)}, u32[]{:S(2)}, u32[]{:S(2)}) async-start(bf16[16,16,256]{2,1,0:T(8,128)(2,1)} %shard_map.102), calls=%async_computation.4 | async-start | bytes 262144 | tf_op jit(solution)/shard_map/all_to_all | solution.py:351
  184.4 1.3 copy-start.1
  187.0 14.1 %collective-permute-start.7 = (bf16[544,256]{1,0:T(8,128)(2,1)S(1)}, bf16[544,256]{1,0:T(8,128)(2,1)S(1)}, u32[]{:S(2)}, u32[]{:S(2)}) collective-permute-start(bf16[544,256]{1,0:T(8,128)(2,1)S(1)} %get-tuple-element.57), channel_id=1, source_target_pairs={{0,4},{4,0},{8,12},{12,8},{1,5},{5,1},{9,13},{13,9},{2,6},{6,2},{1... | collective-permute-start | bytes 835592 | tf_op jit(solution)/shard_map/ppermute | solution.py:348
  189.0 24.2 %collective-permute-start.8 = (bf16[544,256]{1,0:T(8,128)(2,1)S(1)}, bf16[544,256]{1,0:T(8,128)(2,1)S(1)}, u32[]{:S(2)}, u32[]{:S(2)}) collective-permute-start(bf16[544,256]{1,0:T(8,128)(2,1)S(1)} %get-tuple-element.58), channel_id=1, source_target_pairs={{0,8},{4,12},{8,0},{12,4},{1,9},{5,13},{9,1},{13,5},{2,10},{6,14},... | collective-permute-start | bytes 835592 | tf_op jit(solution)/shard_map/ppermute | solution.py:348
  193.8 25.5 %collective-permute-start.9 = (bf16[544,256]{1,0:T(8,128)(2,1)S(1)}, bf16[544,256]{1,0:T(8,128)(2,1)S(1)}, u32[]{:S(2)}, u32[]{:S(2)}) collective-permute-start(bf16[544,256]{1,0:T(8,128)(2,1)S(1)} %get-tuple-element.59), channel_id=1, source_target_pairs={{0,12},{4,8},{8,4},{12,0},{1,13},{5,9},{9,5},{13,1},{2,14},{6,10},... | collective-permute-start | bytes 835592 | tf_op jit(solution)/shard_map/ppermute | solution.py:348
